TPU v7x, 32 devices: a whole 2x2x4 slice. The times are simulated.
32 devices in a mesh: corpus: 4 (over y, x), fsdp: 8 (over z, core).
Axes of the slice: x: 2, y: 2, z: 4, core: 2. Of those that a mesh axis runs over, the one named last changes fastest.
Arguments:
- inputs: bfloat16 [2048, 4096], P('fsdp', 'corpus'), may hold values from -128 to 128
- norm_gain: float32 [4096], replicated, may hold values from 0.1 to 1.9
- w_query: bfloat16 [4096, 8192], P('fsdp', 'corpus'), may hold values from -0.09375 to 0.09375
- w_key: bfloat16 [4096, 1024], P('fsdp', 'corpus'), may hold values from -0.09375 to 0.09375
- w_value: bfloat16 [4096, 1024], P('fsdp', 'corpus'), may hold values from -0.375 to 0.375
- query_bias: float32 [8192], P('corpus'), may hold values from -16 to 16
- key_bias: float32 [1024], P('corpus'), may hold values from -16 to 16
- value_bias: float32 [1024], P('corpus'), may hold values from -4 to 4
- key_cache: bfloat16 [8, 2048, 1024], P('fsdp', None, 'corpus'), may hold values from -16 to 16
- value_cache: bfloat16 [8, 2048, 1024], P('fsdp', None, 'corpus'), may hold values from -16 to 16
- source_doc: int32 [32], P('fsdp'), may hold values from 0 to 7, as said below
- prefix_len: int32 [32], P('fsdp'), may hold values from 1 to 2048
Outputs:
- attention: bfloat16 [2048, 8192], P('fsdp', 'corpus')
Inputs may be any that keep to these rules, and one draw needn't show every extreme that they name: `source_doc`: within the suffixes of one index of fsdp (aligned blocks of 4) no document appears more than 2 times, and one document, drawn from the seed, appears exactly 2 times in every such block.
All inputs are finite; a program needn't handle non-finite values.
Results may differ from a plain program's by a relative error of at most 0.0075.
The roundings to bfloat16 on the way count: a program that leaves them out, or rounds other values in their place, can miss the bound.
Values may be sent and summed in bfloat16 or wider, within the bound.
A program may use at most 128 MiB of HBM per device.

v0:
```python
import jax
import jax.numpy as jnp
from jax import lax
from jax.sharding import PartitionSpec as P

HD = 128
SL = 64
CAP = 2


EPS = 1e-06
THETA = 1000000.0
MASKED = -1e30


def rope_tables(position, width):
    half = width // 2
    freq = THETA ** (-(jnp.arange(half, dtype=jnp.float32) * 2.0 / width))
    angle = position.astype(jnp.float32)[..., None] * freq
    angle = jnp.concatenate([angle, angle], axis=-1)
    return (jnp.cos(angle), jnp.sin(angle))


def rotate(vector, cosine, sine):
    half = vector.shape[-1] // 2
    turned = jnp.concatenate([-vector[..., half:], vector[..., :half]], axis=-1)
    return vector * cosine + turned * sine


def normalize(rows, norm_gain):
    wide = rows.astype(jnp.float32)
    spread = jnp.mean(wide * wide, axis=-1, keepdims=True)
    return (wide * lax.rsqrt(spread + EPS) * norm_gain).astype(jnp.bfloat16)


def partial_attend(query, keys, values, live):
    count = query.shape[0]
    width = query.shape[2]
    length = keys.shape[0]
    kv_heads = keys.shape[1] // width
    group = query.shape[1] // kv_heads
    grouped = query.reshape(count, kv_heads, group, width)
    key_rows = keys.reshape(length, kv_heads, width)
    scores = jnp.einsum(
        "tkgd,lkd->tkgl", grouped, key_rows, preferred_element_type=jnp.float32
    ) * width ** (-0.5)
    scores = jnp.where(live[:, None, None, :], scores, MASKED)
    peak = jnp.max(scores, axis=-1)
    weights = jnp.exp(scores - peak[..., None])
    total = jnp.sum(weights, axis=-1)
    rounded = weights.astype(jnp.bfloat16)
    value_rows = values.reshape(length, kv_heads, width)
    weighted = jnp.einsum("tkgl,lkd->tkgd", rounded, value_rows, preferred_element_type=jnp.float32)
    return (
        weighted.reshape(count, kv_heads * group * width),
        peak.reshape(count, kv_heads * group),
        total.reshape(count, kv_heads * group),
    )


def settle(part):
    weighted, peak, total = part
    shape = peak.shape + (-1,)
    normed = (
        (weighted.reshape(shape) / total[..., None]).reshape(weighted.shape).astype(jnp.bfloat16)
    )
    return (normed, peak + jnp.log(total))


def combine(prefix_normed, prefix_lse, own):
    own_out, own_peak, own_total = own
    top = jnp.maximum(prefix_lse, own_peak)
    scale_first = jnp.exp(prefix_lse - top)
    scale_second = jnp.exp(own_peak - top)
    divisor = scale_first + own_total * scale_second
    shape = own_peak.shape + (-1,)
    mixed = (
        prefix_normed.astype(jnp.float32).reshape(shape) * scale_first[..., None]
        + own_out.reshape(shape) * scale_second[..., None]
    )
    mixed = mixed / divisor[..., None]
    return mixed.reshape(own_peak.shape[:-1] + (-1,)).astype(jnp.bfloat16)


def shards(
    inputs,
    norm_gain,
    w_query,
    w_key,
    w_value,
    query_bias,
    key_bias,
    value_bias,
    key_cache,
    value_cache,
    source_doc,
    prefix_len,
):
    full_rows = lax.all_gather(inputs, "corpus", axis=1, tiled=True)
    normed = normalize(full_rows, norm_gain)
    query_lin = jnp.dot(
        normed,
        lax.all_gather(w_query, "fsdp", axis=0, tiled=True),
        preferred_element_type=jnp.float32,
    )
    key_lin = jnp.dot(
        normed,
        lax.all_gather(w_key, "fsdp", axis=0, tiled=True),
        preferred_element_type=jnp.float32,
    )
    value_lin = jnp.dot(
        normed,
        lax.all_gather(w_value, "fsdp", axis=0, tiled=True),
        preferred_element_type=jnp.float32,
    )
    suffixes = source_doc.shape[0]
    width = HD
    q_heads = w_query.shape[1] // width
    kv_heads = w_key.shape[1] // width
    position = prefix_len[:, None] + jnp.arange(SL, dtype=jnp.int32)[None, :]
    cosine, sine = rope_tables(position, width)
    cosine = cosine[:, :, None, :]
    sine = sine[:, :, None, :]
    queries = rotate(
        (query_lin + query_bias).reshape(suffixes, SL, q_heads, width), cosine, sine
    ).astype(jnp.bfloat16)
    own_keys = rotate(
        (key_lin + key_bias).reshape(suffixes, SL, kv_heads, width), cosine, sine
    ).astype(jnp.bfloat16)
    own_keys = own_keys.reshape(suffixes, SL, kv_heads * width)
    own_values = (
        (value_lin + value_bias).astype(jnp.bfloat16).reshape(suffixes, SL, kv_heads * width)
    )
    causal = jnp.arange(SL, dtype=jnp.int32)[None, :] <= jnp.arange(SL, dtype=jnp.int32)[:, None]
    own_part = jax.vmap(partial_attend, in_axes=(0, 0, 0, None))(
        queries, own_keys, own_values, causal
    )
    documents = lax.axis_size("fsdp")
    slots = documents * CAP
    doc_length = key_cache.shape[1]
    order = jnp.arange(suffixes, dtype=jnp.int32)
    earlier = (source_doc[None, :] == source_doc[:, None]) & (order[None, :] < order[:, None])
    ranking = jnp.sum(earlier.astype(jnp.int32), axis=1)
    slot_of = source_doc * CAP + ranking
    matches = slot_of[None, :] == jnp.arange(slots, dtype=jnp.int32)[:, None]
    holder = jnp.sum(jnp.where(matches, order[None, :], 0), axis=1)
    occupied = jnp.any(matches, axis=1)
    slot_length = jnp.where(occupied, jnp.take(prefix_len, holder, axis=0), 0)
    slot_mask = (jnp.arange(doc_length, dtype=jnp.int32)[None, :] < slot_length[:, None]).astype(
        jnp.bfloat16
    )
    slot_queries = jnp.take(queries, holder, axis=0)
    initial = (
        jnp.zeros((suffixes, SL, q_heads * width), jnp.float32),
        jnp.zeros((suffixes, SL, q_heads), jnp.float32),
        jnp.zeros((suffixes, SL, q_heads), jnp.float32),
    )
    key_piece = lax.all_gather(key_cache, "fsdp", axis=0, tiled=True)
    value_piece = lax.all_gather(value_cache, "fsdp", axis=0, tiled=True)
    count = key_piece.shape[0]

    def one_document(item):
        doc_queries, doc_masks, doc_keys, doc_values = item
        live = jnp.broadcast_to(doc_masks[:, None, :] > 0, (CAP, SL, doc_masks.shape[-1]))
        return jax.vmap(partial_attend, in_axes=(0, None, None, 0))(
            doc_queries, doc_keys, doc_values, live
        )

    results = lax.map(
        one_document,
        (
            slot_queries.reshape((count, CAP) + slot_queries.shape[1:]),
            slot_mask.reshape(count, CAP, doc_length),
            key_piece,
            value_piece,
        ),
    )
    results = tuple((part.reshape((count * CAP,) + part.shape[2:]) for part in results))
    inside = (slot_of >= 0) & (slot_of < count * CAP)
    chosen = jnp.clip(slot_of, 0, count * CAP - 1)
    gathered_part = tuple(
        (
            jnp.where(inside[:, None, None], jnp.take(fresh, chosen, axis=0), older)
            for older, fresh in zip(initial, results)
        )
    )
    prefix_normed, prefix_lse = settle(gathered_part)
    attention = combine(prefix_normed, prefix_lse, own_part)
    return attention.reshape(suffixes * SL, q_heads * width)


def solution(mesh):
    in_specs = (
        P("fsdp", "corpus"),
        P(),
        P("fsdp", "corpus"),
        P("fsdp", "corpus"),
        P("fsdp", "corpus"),
        P("corpus"),
        P("corpus"),
        P("corpus"),
        P("fsdp", None, "corpus"),
        P("fsdp", None, "corpus"),
        P("fsdp"),
        P("fsdp"),
    )
    out_specs = P("fsdp", "corpus")
    return jax.shard_map(shards, mesh=mesh, in_specs=in_specs, out_specs=out_specs, check_vma=False)
```

profile of v0, /device:TPU:0, one launch (start us, length us, event | category | flops | bytes accessed | tf_op | source)
XLA Modules:
  0.0 685.7 jit_solution(6007420988527938023)
XLA Ops:
  15.4 31.9 %all-gather.11.cloned.1.call-done = bf16[256,4096]{1,0:T(8,128)(2,1)} async-done(((bf16[256,1024]{1,0:T(8,128)(2,1)}), bf16[256,4096]{1,0:T(8,128)(2,1)}) %all-gather.11.cloned.1.call-update) | async-done | bytes 2097168 | tf_op jit(solution)/shard_map/all_gather | solution.py:99
  49.5 28.5 %all-gather.15.cloned.1.call-done = bf16[4096,256]{1,0:T(8,128)(2,1)} async-done(((bf16[512,256]{1,0:T(8,128)(2,1)}), bf16[4096,256]{1,0:T(8,128)(2,1)}) %all-gather.15.cloned.1.call-update) | async-done | bytes 2097168 | tf_op jit(solution)/shard_map/all_gather | solution.py:108
  80.5 27.7 %all-gather.17.cloned.1.call-done = bf16[4096,256]{1,0:T(8,128)(2,1)} async-done(((bf16[512,256]{1,0:T(8,128)(2,1)}), bf16[4096,256]{1,0:T(8,128)(2,1)}) %all-gather.17.cloned.1.call-update) | async-done | bytes 2097168 | tf_op jit(solution)/shard_map/all_gather | solution.py:113
  110.8 149.5 %all-gather.13.cloned.1.call-done = bf16[4096,2048]{1,0:T(8,128)(2,1)} async-done(((bf16[512,2048]{1,0:T(8,128)(2,1)}), bf16[4096,2048]{1,0:T(8,128)(2,1)}) %all-gather.13.cloned.1.call-update) | async-done | bytes 16777232 | tf_op jit(solution)/shard_map/all_gather | solution.py:103
  260.3 8.2 %fusion.26 = f32[32,8,16,128]{3,1,2,0:T(8,128)S(1)} fusion(bf16[4096,2048]{1,0:T(8,128)(2,1)} %all-gather.13.cloned.1.call-done, f32[2048]{0:T(1024)S(1)} %copy-done.18, bf16[256,4096]{1,0:T(8,128)(2,1)S(1)} %copy-done.7, f32[4096]{0:T(1024)S(1)} %copy-done.17, f32[256]{0:T(256)S(1)} %add_rsqrt_fusion), kind=kOutput, calls=%fused_computation.52 | convolution fusion | flops 4299685888 | bytes 20997120 | tf_op jit(solution)/shard_map/dot_general | solution.py:101
  291.7 50.4 %all-gather.9.cloned.1.call-done = bf16[8,2048,256]{2,1,0:T(8,128)(2,1)} async-done(((bf16[1,2048,256]{2,1,0:T(8,128)(2,1)}), bf16[8,2048,256]{2,1,0:T(8,128)(2,1)}) %all-gather.9.cloned.1.call-update) | async-done | bytes 8388624 | tf_op jit(solution)/shard_map/all_gather | solution.py:158
  342.1 82.1 %all-gather.7.cloned.1.call-done = bf16[8,2048,256]{2,1,0:T(8,128)(2,1)} async-done(((bf16[1,2048,256]{2,1,0:T(8,128)(2,1)}), bf16[8,2048,256]{2,1,0:T(8,128)(2,1)}) %all-gather.7.cloned.1.call-update) | async-done | bytes 8388624 | tf_op jit(solution)/shard_map/all_gather | solution.py:159
  424.2 241.4 %while.14 = (s32[]{:T(128)}, f32[8,2,64,2048]{3,2,1,0:T(8,128)}, f32[8,2,64,16]{2,3,1,0:T(8,128)S(1)}, f32[8,2,64,16]{2,3,1,0:T(8,128)S(1)}, bf16[8,2048,256]{2,...) while((s32[]{:T(128)}, f32[8,2,64,2048]{3,2,1,0:T(8,128)}, ...), condition=%wide.region_7.8_spmd, body=%wide.region_4.0_spmd.sunk | while | flops 2193620992 | bytes 74047632 | solution.py:169
  437.1 7.6 %fusion.72 = f32[2,64,2,8,128]{4,1,3,0,2:T(8,128)S(1)} fusion(bf16[2048,2,128,1,1]{0,2,4,3,1:T(8,128)(2,1)S(1)} %bitcast.142, f32[2,2048,2,64,8]{1,3,4,2,0:T(8,128)} %get-tuple-element.168, f32[2,64,2,8]{1,3,0,2:T(8,128)S(1)} %get-tuple-element.169, pred[2,2048]{1,0:T(4,128)(4,1)S(1)} %compare_bitcast_fusion.2), kind=kOutput, calls=%fused_computation.12.clone.1 | convolution fusion | flops 1090519040 | bytes 18886656 | tf_op jit(solution)/shard_map/while/body/eval_jaxpr/vmap(tkgl,lkd->tkgd)/dot_general | solution.py:53
  444.6 7.8 %fusion.73 = f32[2,64,2,8]{1,3,0,2:T(8,128)S(1)} fusion(f32[2,2048,2,64,8]{1,3,4,2,0:T(8,128)} %get-tuple-element.168, f32[2,64,2,8]{1,3,0,2:T(8,128)S(1)} %get-tuple-element.169, pred[2,2048]{1,0:T(4,128)(4,1)S(1)} %compare_bitcast_fusion.2), kind=kLoop, calls=%fused_computation.7.clone.1 | loop fusion | flops 16775168 | bytes 16797696 | tf_op jit(solution)/shard_map/while/body/eval_jaxpr/vmap()/reduce_sum | solution.py:50
  467.2 7.6 %fusion.72 = f32[2,64,2,8,128]{4,1,3,0,2:T(8,128)S(1)} fusion(bf16[2048,2,128,1,1]{0,2,4,3,1:T(8,128)(2,1)S(1)} %bitcast.142, f32[2,2048,2,64,8]{1,3,4,2,0:T(8,128)} %get-tuple-element.168, f32[2,64,2,8]{1,3,0,2:T(8,128)S(1)} %get-tuple-element.169, pred[2,2048]{1,0:T(4,128)(4,1)S(1)} %compare_bitcast_fusion.2), kind=kOutput, calls=%fused_computation.12.clone.1 | convolution fusion | flops 1090519040 | bytes 18886656 | tf_op jit(solution)/shard_map/while/body/eval_jaxpr/vmap(tkgl,lkd->tkgd)/dot_general | solution.py:53
  474.8 7.8 %fusion.73 = f32[2,64,2,8]{1,3,0,2:T(8,128)S(1)} fusion(f32[2,2048,2,64,8]{1,3,4,2,0:T(8,128)} %get-tuple-element.168, f32[2,64,2,8]{1,3,0,2:T(8,128)S(1)} %get-tuple-element.169, pred[2,2048]{1,0:T(4,128)(4,1)S(1)} %compare_bitcast_fusion.2), kind=kLoop, calls=%fused_computation.7.clone.1 | loop fusion | flops 16775168 | bytes 16797696 | tf_op jit(solution)/shard_map/while/body/eval_jaxpr/vmap()/reduce_sum | solution.py:50
  497.4 7.6 %fusion.72 = f32[2,64,2,8,128]{4,1,3,0,2:T(8,128)S(1)} fusion(bf16[2048,2,128,1,1]{0,2,4,3,1:T(8,128)(2,1)S(1)} %bitcast.142, f32[2,2048,2,64,8]{1,3,4,2,0:T(8,128)} %get-tuple-element.168, f32[2,64,2,8]{1,3,0,2:T(8,128)S(1)} %get-tuple-element.169, pred[2,2048]{1,0:T(4,128)(4,1)S(1)} %compare_bitcast_fusion.2), kind=kOutput, calls=%fused_computation.12.clone.1 | convolution fusion | flops 1090519040 | bytes 18886656 | tf_op jit(solution)/shard_map/while/body/eval_jaxpr/vmap(tkgl,lkd->tkgd)/dot_general | solution.py:53
  505.0 7.8 %fusion.73 = f32[2,64,2,8]{1,3,0,2:T(8,128)S(1)} fusion(f32[2,2048,2,64,8]{1,3,4,2,0:T(8,128)} %get-tuple-element.168, f32[2,64,2,8]{1,3,0,2:T(8,128)S(1)} %get-tuple-element.169, pred[2,2048]{1,0:T(4,128)(4,1)S(1)} %compare_bitcast_fusion.2), kind=kLoop, calls=%fused_computation.7.clone.1 | loop fusion | flops 16775168 | bytes 16797696 | tf_op jit(solution)/shard_map/while/body/eval_jaxpr/vmap()/reduce_sum | solution.py:50
  527.6 7.6 %fusion.72 = f32[2,64,2,8,128]{4,1,3,0,2:T(8,128)S(1)} fusion(bf16[2048,2,128,1,1]{0,2,4,3,1:T(8,128)(2,1)S(1)} %bitcast.142, f32[2,2048,2,64,8]{1,3,4,2,0:T(8,128)} %get-tuple-element.168, f32[2,64,2,8]{1,3,0,2:T(8,128)S(1)} %get-tuple-element.169, pred[2,2048]{1,0:T(4,128)(4,1)S(1)} %compare_bitcast_fusion.2), kind=kOutput, calls=%fused_computation.12.clone.1 | convolution fusion | flops 1090519040 | bytes 18886656 | tf_op jit(solution)/shard_map/while/body/eval_jaxpr/vmap(tkgl,lkd->tkgd)/dot_general | solution.py:53
  535.1 7.8 %fusion.73 = f32[2,64,2,8]{1,3,0,2:T(8,128)S(1)} fusion(f32[2,2048,2,64,8]{1,3,4,2,0:T(8,128)} %get-tuple-element.168, f32[2,64,2,8]{1,3,0,2:T(8,128)S(1)} %get-tuple-element.169, pred[2,2048]{1,0:T(4,128)(4,1)S(1)} %compare_bitcast_fusion.2), kind=kLoop, calls=%fused_computation.7.clone.1 | loop fusion | flops 16775168 | bytes 16797696 | tf_op jit(solution)/shard_map/while/body/eval_jaxpr/vmap()/reduce_sum | solution.py:50
  557.7 7.6 %fusion.72 = f32[2,64,2,8,128]{4,1,3,0,2:T(8,128)S(1)} fusion(bf16[2048,2,128,1,1]{0,2,4,3,1:T(8,128)(2,1)S(1)} %bitcast.142, f32[2,2048,2,64,8]{1,3,4,2,0:T(8,128)} %get-tuple-element.168, f32[2,64,2,8]{1,3,0,2:T(8,128)S(1)} %get-tuple-element.169, pred[2,2048]{1,0:T(4,128)(4,1)S(1)} %compare_bitcast_fusion.2), kind=kOutput, calls=%fused_computation.12.clone.1 | convolution fusion | flops 1090519040 | bytes 18886656 | tf_op jit(solution)/shard_map/while/body/eval_jaxpr/vmap(tkgl,lkd->tkgd)/dot_general | solution.py:53
  565.3 7.8 %fusion.73 = f32[2,64,2,8]{1,3,0,2:T(8,128)S(1)} fusion(f32[2,2048,2,64,8]{1,3,4,2,0:T(8,128)} %get-tuple-element.168, f32[2,64,2,8]{1,3,0,2:T(8,128)S(1)} %get-tuple-element.169, pred[2,2048]{1,0:T(4,128)(4,1)S(1)} %compare_bitcast_fusion.2), kind=kLoop, calls=%fused_computation.7.clone.1 | loop fusion | flops 16775168 | bytes 16797696 | tf_op jit(solution)/shard_map/while/body/eval_jaxpr/vmap()/reduce_sum | solution.py:50
  587.9 7.6 %fusion.72 = f32[2,64,2,8,128]{4,1,3,0,2:T(8,128)S(1)} fusion(bf16[2048,2,128,1,1]{0,2,4,3,1:T(8,128)(2,1)S(1)} %bitcast.142, f32[2,2048,2,64,8]{1,3,4,2,0:T(8,128)} %get-tuple-element.168, f32[2,64,2,8]{1,3,0,2:T(8,128)S(1)} %get-tuple-element.169, pred[2,2048]{1,0:T(4,128)(4,1)S(1)} %compare_bitcast_fusion.2), kind=kOutput, calls=%fused_computation.12.clone.1 | convolution fusion | flops 1090519040 | bytes 18886656 | tf_op jit(solution)/shard_map/while/body/eval_jaxpr/vmap(tkgl,lkd->tkgd)/dot_general | solution.py:53
  595.5 7.8 %fusion.73 = f32[2,64,2,8]{1,3,0,2:T(8,128)S(1)} fusion(f32[2,2048,2,64,8]{1,3,4,2,0:T(8,128)} %get-tuple-element.168, f32[2,64,2,8]{1,3,0,2:T(8,128)S(1)} %get-tuple-element.169, pred[2,2048]{1,0:T(4,128)(4,1)S(1)} %compare_bitcast_fusion.2), kind=kLoop, calls=%fused_computation.7.clone.1 | loop fusion | flops 16775168 | bytes 16797696 | tf_op jit(solution)/shard_map/while/body/eval_jaxpr/vmap()/reduce_sum | solution.py:50
  618.1 7.6 %fusion.72 = f32[2,64,2,8,128]{4,1,3,0,2:T(8,128)S(1)} fusion(bf16[2048,2,128,1,1]{0,2,4,3,1:T(8,128)(2,1)S(1)} %bitcast.142, f32[2,2048,2,64,8]{1,3,4,2,0:T(8,128)} %get-tuple-element.168, f32[2,64,2,8]{1,3,0,2:T(8,128)S(1)} %get-tuple-element.169, pred[2,2048]{1,0:T(4,128)(4,1)S(1)} %compare_bitcast_fusion.2), kind=kOutput, calls=%fused_computation.12.clone.1 | convolution fusion | flops 1090519040 | bytes 18886656 | tf_op jit(solution)/shard_map/while/body/eval_jaxpr/vmap(tkgl,lkd->tkgd)/dot_general | solution.py:53
  625.7 7.8 %fusion.73 = f32[2,64,2,8]{1,3,0,2:T(8,128)S(1)} fusion(f32[2,2048,2,64,8]{1,3,4,2,0:T(8,128)} %get-tuple-element.168, f32[2,64,2,8]{1,3,0,2:T(8,128)S(1)} %get-tuple-element.169, pred[2,2048]{1,0:T(4,128)(4,1)S(1)} %compare_bitcast_fusion.2), kind=kLoop, calls=%fused_computation.7.clone.1 | loop fusion | flops 16775168 | bytes 16797696 | tf_op jit(solution)/shard_map/while/body/eval_jaxpr/vmap()/reduce_sum | solution.py:50
  648.2 7.6 %fusion.72 = f32[2,64,2,8,128]{4,1,3,0,2:T(8,128)S(1)} fusion(bf16[2048,2,128,1,1]{0,2,4,3,1:T(8,128)(2,1)S(1)} %bitcast.142, f32[2,2048,2,64,8]{1,3,4,2,0:T(8,128)} %get-tuple-element.168, f32[2,64,2,8]{1,3,0,2:T(8,128)S(1)} %get-tuple-element.169, pred[2,2048]{1,0:T(4,128)(4,1)S(1)} %compare_bitcast_fusion.2), kind=kOutput, calls=%fused_computation.12.clone.1 | convolution fusion | flops 1090519040 | bytes 18886656 | tf_op jit(solution)/shard_map/while/body/eval_jaxpr/vmap(tkgl,lkd->tkgd)/dot_general | solution.py:53
  655.8 7.8 %fusion.73 = f32[2,64,2,8]{1,3,0,2:T(8,128)S(1)} fusion(f32[2,2048,2,64,8]{1,3,4,2,0:T(8,128)} %get-tuple-element.168, f32[2,64,2,8]{1,3,0,2:T(8,128)S(1)} %get-tuple-element.169, pred[2,2048]{1,0:T(4,128)(4,1)S(1)} %compare_bitcast_fusion.2), kind=kLoop, calls=%fused_computation.7.clone.1 | loop fusion | flops 16775168 | bytes 16797696 | tf_op jit(solution)/shard_map/while/body/eval_jaxpr/vmap()/reduce_sum | solution.py:50
  (215 shorter events, 170.1 us)
Async XLA Ops:
  6.5 40.7 %all-gather.11.cloned.1.call-start = ((), (), s32[]{:S(2)}) async-start(), calls=%async_computation.2 | async-start | bytes 2621440 | tf_op jit(solution)/shard_map/all_gather | solution.py:99
  7.3 70.7 %all-gather.15.cloned.1.call-start = ((), (), s32[]{:S(2)}) async-start(), calls=%async_computation.4 | async-start | bytes 2359296 | tf_op jit(solution)/shard_map/all_gather | solution.py:108
  8.0 100.2 %all-gather.17.cloned.1.call-start = ((), (), s32[]{:S(2)}) async-start(), calls=%async_computation.5 | async-start | bytes 2359296 | tf_op jit(solution)/shard_map/all_gather | solution.py:113
  8.8 4.3 copy-start
  8.8 251.5 %all-gather.13.cloned.1.call-start = ((), (), s32[]{:S(2)}) async-start(), calls=%async_computation.3 | async-start | bytes 18874368 | tf_op jit(solution)/shard_map/all_gather | solution.py:103
  9.3 332.7 %all-gather.9.cloned.1.call-start = ((), (), s32[]{:S(2)}) async-start(), calls=%async_computation.1 | async-start | bytes 9437184 | tf_op jit(solution)/shard_map/all_gather | solution.py:158
  9.9 68.1 %copy-start.17 = (f32[4096]{0:T(1024)S(1)}, f32[4096]{0:T(1024)}, u32[]{:S(2)}) copy-start(f32[4096]{0:T(1024)} %param.17) | copy-start | bytes 49156
  9.9 68.1 %copy-start.19 = (f32[256]{0:T(256)S(1)}, f32[256]{0:T(256)}, u32[]{:S(2)}) copy-start(f32[256]{0:T(256)} %param.22) | copy-start | bytes 3076
  9.9 414.2 %all-gather.7.cloned.1.call-start = ((), (), s32[]{:S(2)}) async-start(), calls=%async_computation | async-start | bytes 9437184 | tf_op jit(solution)/shard_map/all_gather | solution.py:159
  47.3 30.7 %copy-start.7 = (bf16[256,4096]{1,0:T(8,128)(2,1)S(1)}, bf16[256,4096]{1,0:T(8,128)(2,1)}, u32[]{:S(2)}) copy-start(bf16[256,4096]{1,0:T(8,128)(2,1)} %all-gather.11.cloned.1.call-done) | copy-start | bytes 6291460
  49.5 58.7 %copy-start.20 = (f32[256]{0:T(256)S(1)}, f32[256]{0:T(256)}, u32[]{:S(2)}) copy-start(f32[256]{0:T(256)} %param.23) | copy-start | bytes 3076
  80.5 179.8 %copy-start.18 = (f32[2048]{0:T(1024)S(1)}, f32[2048]{0:T(1024)}, u32[]{:S(2)}) copy-start(f32[2048]{0:T(1024)} %param.21) | copy-start | bytes 24580
  287.0 137.1 %copy-start.8 = (f32[8,2,64,16]{2,3,1,0:T(8,128)S(1)}, f32[8,2,64,16]{2,3,1,0:T(8,128)}, u32[]{:S(2)}) copy-start(f32[8,2,64,16]{2,3,1,0:T(8,128)} %custom-call.12) | copy-start | bytes 196612
  287.0 137.1 %copy-start.9 = (f32[8,2,64,16]{2,3,1,0:T(8,128)S(1)}, f32[8,2,64,16]{2,3,1,0:T(8,128)}, u32[]{:S(2)}) copy-start(f32[8,2,64,16]{2,3,1,0:T(8,128)} %custom-call.11) | copy-start | bytes 196612
  429.9 7.1 %copy-start.1 = (bf16[1,2048,256]{1,2,0:T(8,128)(2,1)S(1)}, bf16[1,2048,256]{1,2,0:T(8,128)(2,1)}, u32[]{:S(2)}) copy-start(bf16[1,2048,256]{1,2,0:T(8,128)(2,1)} %copy.160) | copy-start | bytes 3145732 | tf_op jit(solution)/shard_map/while
  460.1 7.1 %copy-start.1 = (bf16[1,2048,256]{1,2,0:T(8,128)(2,1)S(1)}, bf16[1,2048,256]{1,2,0:T(8,128)(2,1)}, u32[]{:S(2)}) copy-start(bf16[1,2048,256]{1,2,0:T(8,128)(2,1)} %copy.160) | copy-start | bytes 3145732 | tf_op jit(solution)/shard_map/while
  490.3 7.1 %copy-start.1 = (bf16[1,2048,256]{1,2,0:T(8,128)(2,1)S(1)}, bf16[1,2048,256]{1,2,0:T(8,128)(2,1)}, u32[]{:S(2)}) copy-start(bf16[1,2048,256]{1,2,0:T(8,128)(2,1)} %copy.160) | copy-start | bytes 3145732 | tf_op jit(solution)/shard_map/while
  520.4 7.1 %copy-start.1 = (bf16[1,2048,256]{1,2,0:T(8,128)(2,1)S(1)}, bf16[1,2048,256]{1,2,0:T(8,128)(2,1)}, u32[]{:S(2)}) copy-start(bf16[1,2048,256]{1,2,0:T(8,128)(2,1)} %copy.160) | copy-start | bytes 3145732 | tf_op jit(solution)/shard_map/while
  550.6 7.1 %copy-start.1 = (bf16[1,2048,256]{1,2,0:T(8,128)(2,1)S(1)}, bf16[1,2048,256]{1,2,0:T(8,128)(2,1)}, u32[]{:S(2)}) copy-start(bf16[1,2048,256]{1,2,0:T(8,128)(2,1)} %copy.160) | copy-start | bytes 3145732 | tf_op jit(solution)/shard_map/while
  580.8 7.1 %copy-start.1 = (bf16[1,2048,256]{1,2,0:T(8,128)(2,1)S(1)}, bf16[1,2048,256]{1,2,0:T(8,128)(2,1)}, u32[]{:S(2)}) copy-start(bf16[1,2048,256]{1,2,0:T(8,128)(2,1)} %copy.160) | copy-start | bytes 3145732 | tf_op jit(solution)/shard_map/while
  611.0 7.1 %copy-start.1 = (bf16[1,2048,256]{1,2,0:T(8,128)(2,1)S(1)}, bf16[1,2048,256]{1,2,0:T(8,128)(2,1)}, u32[]{:S(2)}) copy-start(bf16[1,2048,256]{1,2,0:T(8,128)(2,1)} %copy.160) | copy-start | bytes 3145732 | tf_op jit(solution)/shard_map/while
  641.1 7.1 %copy-start.1 = (bf16[1,2048,256]{1,2,0:T(8,128)(2,1)S(1)}, bf16[1,2048,256]{1,2,0:T(8,128)(2,1)}, u32[]{:S(2)}) copy-start(bf16[1,2048,256]{1,2,0:T(8,128)(2,1)} %copy.160) | copy-start | bytes 3145732 | tf_op jit(solution)/shard_map/while
  666.2 4.9 copy-start.11
  666.2 4.9 copy-start.15
  (10 other events, 18.0 us)
Sparse Core Ops, SparseCore 0:
  9.2 38.0 all-gather.10
  48.8 29.0 all-gather.14
  79.6 28.5 all-gather.16
  109.7 150.5 all-gather.12
  261.7 80.2 all-gather.8
  343.5 80.5 all-gather.6
where the time goes:
time: 687 us; the launch traced here: 686 us
  waiting for transfers between devices  374 us (54%)
  matrix products  133 us (19%)
  local copies, waits for them, and re-layouts  84.7 us (12%)
  other arithmetic  80.2 us (12%)
  between operations  13.9 us (2%)
    all_gather x1, waiting for transfers between devices, shards(): lax.all_gather(w_query, 'fsdp', axis=0, tiled=True)  150 us
    all_gather x1, waiting for transfers between devices, shards(): value_piece = lax.all_gather(value_cache, 'fsdp', axis=0, tiled=True)  82.1 us
    reduce_sum x9, other arithmetic, partial_attend(): total = jnp.sum(weights, axis=-1)  63 us
    dot_general x9, matrix products, partial_attend(): jnp.einsum('tkgl,lkd->tkgd', rounded, value_rows, preferred_element_type=...  61.1 us
    dot_general x9, matrix products, partial_attend(): jnp.einsum('tkgd,lkd->tkgl', grouped, key_rows, preferred_element_type=jn...  58.6 us
    all_gather x1, waiting for transfers between devices, shards(): key_piece = lax.all_gather(key_cache, 'fsdp', axis=0, tiled=True)  50.4 us
    dynamic_slice x32, local copies, waits for them, and re-layouts, shards(): lax.map(one_document, (slot_queries.reshape((count, CAP) + slot_queries.s...  37.3 us
    all_gather x1, waiting for transfers between devices, shards(): full_rows = lax.all_gather(inputs, 'corpus', axis=1, tiled=True)  31.9 us
  transfers between devices with their start and end apart: 6, of which 6 were waited for; matrix products, arithmetic and copies ran while one was open for 6% of the time, Pallas kernels for 0%

commit v1 on v0

v1 whole, which is shorter than its diff:
```python
import jax
import jax.numpy as jnp
from jax import lax
from jax.experimental import pallas as pl
from jax.experimental.pallas import tpu as pltpu
from jax.sharding import PartitionSpec as P

HD = 128
SL = 64
EPS = 1e-06
THETA = 1000000.0
MASKED = -1e30
KEY_BLOCK = 512


def rope_tables(position, width):
    half = width // 2
    freq = THETA ** (-(jnp.arange(half, dtype=jnp.float32) * 2.0 / width))
    angle = position.astype(jnp.float32)[..., None] * freq
    cosine, sine = jnp.cos(angle), jnp.sin(angle)
    return (
        jnp.concatenate([cosine, cosine], axis=-1),
        jnp.concatenate([-sine, sine], axis=-1),
    )


def normalize(rows, norm_gain):
    wide = rows.astype(jnp.float32)
    spread = jnp.mean(wide * wide, axis=-1, keepdims=True)
    return (wide * lax.rsqrt(spread + EPS) * norm_gain).astype(jnp.bfloat16)


def rotate(vector, cosine, sine):
    return vector * cosine + pltpu.roll(vector, HD // 2, 1) * sine


def over_lanes(op, array):
    parts = [array[:, at : at + 128] for at in range(0, array.shape[1], 128)]
    while len(parts) > 1:
        parts = [op(a, b) for a, b in zip(parts[::2], parts[1::2])]
    return parts[0]


def attend_kernel(
    doc_ref,
    len_ref,
    q_ref,
    k_ref,
    v_ref,
    qb_ref,
    kb_ref,
    vb_ref,
    cos_ref,
    sin_ref,
    keys_ref,
    values_ref,
    out_ref,
    scores_ref,
    queries_ref,
    peak_ref,
    total_ref,
    acc_ref,
):
    suffix = pl.program_id(0)
    length = len_ref[suffix]
    scale = HD ** (-0.5)
    group = q_ref.shape[1] // HD
    rows = group * SL
    cosine = cos_ref[...]
    sine = sin_ref[...]
    lin = q_ref[...] + qb_ref[...]
    for h in range(group):
        queries_ref[h * SL : (h + 1) * SL, :] = rotate(
            lin[:, h * HD : (h + 1) * HD], cosine, sine
        ).astype(jnp.bfloat16)
    own_keys = rotate(k_ref[...] + kb_ref[...], cosine, sine).astype(jnp.bfloat16)
    own_values = (v_ref[...] + vb_ref[...]).astype(jnp.bfloat16)
    dims = (((1,), (1,)), ((), ()))

    block = KEY_BLOCK
    blocks = lax.div(length + (block - 1), block)
    peak_ref[...] = jnp.full(peak_ref.shape, MASKED, jnp.float32)

    @pl.loop(0, blocks)
    def _(b):
        at = pl.multiple_of(b * block, block)
        scores = lax.dot_general(
            queries_ref[...],
            keys_ref[0, pl.ds(at, block), :],
            dims,
            preferred_element_type=jnp.float32,
        ) * scale
        column = lax.broadcasted_iota(jnp.int32, (1, block), 1) + at
        scores = jnp.where(column < length, scores, MASKED)
        scores_ref[b] = scores
        peak_ref[...] = jnp.maximum(peak_ref[...], over_lanes(jnp.maximum, scores))

    peak = jnp.max(peak_ref[...], axis=1, keepdims=True)
    peak_ref[...] = jnp.broadcast_to(peak, peak_ref.shape)
    total_ref[...] = jnp.zeros_like(total_ref)
    acc_ref[...] = jnp.zeros_like(acc_ref)

    @pl.loop(0, blocks)
    def _(b):
        at = pl.multiple_of(b * block, block)
        weights = jnp.exp(scores_ref[b] - jnp.tile(peak_ref[...], (1, block // 128)))
        total_ref[...] += over_lanes(jnp.add, weights)
        acc_ref[...] += jnp.dot(
            weights.astype(jnp.bfloat16),
            values_ref[0, pl.ds(at, block), :],
            preferred_element_type=jnp.float32,
        )

    total = jnp.sum(total_ref[...], axis=1, keepdims=True)
    prefix_normed = (acc_ref[...] / total).astype(jnp.bfloat16)
    prefix_lse = peak_ref[...][:, :1] + jnp.log(total)

    own = lax.dot_general(
        queries_ref[...], own_keys, dims, preferred_element_type=jnp.float32
    ) * scale
    token = lax.rem(lax.broadcasted_iota(jnp.int32, (rows, SL), 0), SL)
    other = lax.broadcasted_iota(jnp.int32, (rows, SL), 1)
    own = jnp.where(other <= token, own, MASKED)
    own_peak = jnp.max(own, axis=1, keepdims=True)
    own_weights = jnp.exp(own - own_peak)
    own_total = jnp.sum(own_weights, axis=1, keepdims=True)
    own_out = jnp.dot(
        own_weights.astype(jnp.bfloat16), own_values, preferred_element_type=jnp.float32
    )
    top = jnp.maximum(prefix_lse, own_peak)
    first = jnp.exp(prefix_lse - top)
    second = jnp.exp(own_peak - top)
    divisor = first + own_total * second
    mixed = (prefix_normed.astype(jnp.float32) * first + own_out * second) / divisor
    mixed = mixed.astype(jnp.bfloat16)
    for h in range(group):
        out_ref[:, h * HD : (h + 1) * HD] = mixed[h * SL : (h + 1) * SL, :]


def attend(source_doc, prefix_len, q_lin, k_lin, v_lin, q_bias, k_bias, v_bias, cosine, sine, keys, values):
    suffixes = source_doc.shape[0]
    kv_heads = k_lin.shape[1] // HD
    wide = q_lin.shape[1] // kv_heads
    rows = wide // HD * SL
    length = keys.shape[1]
    block = pl.BlockSpec
    per_head = lambda i, g, doc, size: (i, g)
    bias = lambda i, g, doc, size: (0, g)
    table = lambda i, g, doc, size: (i, 0)
    cached = lambda i, g, doc, size: (doc[i], 0, g)
    flops = 4 * suffixes * kv_heads * rows * length * HD
    return pl.pallas_call(
        attend_kernel,
        out_shape=jax.ShapeDtypeStruct(q_lin.shape, jnp.bfloat16),
        grid_spec=pltpu.PrefetchScalarGridSpec(
            num_scalar_prefetch=2,
            grid=(suffixes, kv_heads),
            in_specs=[
                block((SL, wide), per_head),
                block((SL, HD), per_head),
                block((SL, HD), per_head),
                block((1, wide), bias),
                block((1, HD), bias),
                block((1, HD), bias),
                block((SL, HD), table),
                block((SL, HD), table),
                block((1, length, HD), cached),
                block((1, length, HD), cached),
            ],
            out_specs=block((SL, wide), per_head),
            scratch_shapes=[
                pltpu.VMEM((length // KEY_BLOCK, rows, KEY_BLOCK), jnp.float32),
                pltpu.VMEM((rows, HD), jnp.bfloat16),
                pltpu.VMEM((rows, 128), jnp.float32),
                pltpu.VMEM((rows, 128), jnp.float32),
                pltpu.VMEM((rows, HD), jnp.float32),
            ],
        ),
        compiler_params=pltpu.CompilerParams(
            dimension_semantics=("arbitrary", "arbitrary"), vmem_limit_bytes=40 << 20
        ),
        cost_estimate=pl.CostEstimate(
            flops=flops, transcendentals=flops // (4 * HD), bytes_accessed=16 << 20
        ),
    )(source_doc, prefix_len, q_lin, k_lin, v_lin, q_bias[None], k_bias[None], v_bias[None], cosine, sine, keys, values)


def shards(
    inputs,
    norm_gain,
    w_query,
    w_key,
    w_value,
    query_bias,
    key_bias,
    value_bias,
    key_cache,
    value_cache,
    source_doc,
    prefix_len,
):
    full_rows = lax.all_gather(inputs, "corpus", axis=1, tiled=True)
    normed = normalize(full_rows, norm_gain)

    def project(weight):
        whole = lax.all_gather(weight, "fsdp", axis=0, tiled=True)
        return jnp.dot(normed, whole, preferred_element_type=jnp.float32)

    q_lin, k_lin, v_lin = project(w_query), project(w_key), project(w_value)
    keys = lax.all_gather(key_cache, "fsdp", axis=0, tiled=True)
    values = lax.all_gather(value_cache, "fsdp", axis=0, tiled=True)
    position = prefix_len[:, None] + jnp.arange(SL, dtype=jnp.int32)[None, :]
    cosine, sine = rope_tables(position.reshape(-1), HD)
    return attend(
        source_doc, prefix_len, q_lin, k_lin, v_lin, query_bias, key_bias, value_bias, cosine, sine, keys, values
    )


def solution(mesh):
    in_specs = (
        P("fsdp", "corpus"),
        P(),
        P("fsdp", "corpus"),
        P("fsdp", "corpus"),
        P("fsdp", "corpus"),
        P("corpus"),
        P("corpus"),
        P("corpus"),
        P("fsdp", None, "corpus"),
        P("fsdp", None, "corpus"),
        P("fsdp"),
        P("fsdp"),
    )
    out_specs = P("fsdp", "corpus")
    return jax.shard_map(shards, mesh=mesh, in_specs=in_specs, out_specs=out_specs, check_vma=False)
```

time: 687 us -> 465 us (0.68)
  matrix products: 133 us -> 13.6 us
  local copies, waits for them, and re-layouts: 84.7 us -> 3.5 us
  other arithmetic: 80.2 us -> 3 us
  Pallas kernels: 0 us -> 28.7 us
  waiting for transfers between devices: 374 us -> 401 us
    dot_general x21 -> x3, matrix products: 133 us -> 13.6 us  [project(): return jnp.dot(normed, whole, preferred_element_type=jnp.float32)]
    reduce_sum x11 -> x0, other arithmetic: 63.2 us -> none  [the longest x9 63 us: partial_attend(): total = jnp.sum(weights, axis=-1)]
    dynamic_slice x32 -> x0, local copies, waits for them, and re-layouts: 37.3 us -> none  [shards(): lax.map(one_document, (slot_queries.reshape((count, CAP) + slot_queries.s...]
    pallas_call x0 -> x1, Pallas kernels: none -> 28.7 us  [attend(): pl.pallas_call(attend_kernel, out_shape=jax.ShapeDtypeStruct(q_lin.shape,...]
    all_gather x5, waiting for transfers between devices: 338 us -> 361 us  [the longest x3 206 us: project(): whole = lax.all_gather(weight, 'fsdp', axis=0, tiled=True)]
    reshape x11 -> x0, local copies, waits for them, and re-layouts: 11.5 us -> none  [the longest x8 8.67 us: partial_attend(): grouped = query.reshape(count, kv_heads, group, width)]
    gather x6 -> x0, local copies, waits for them, and re-layouts: 9.29 us -> none  [the longest x3 5.53 us: shards(): jnp.take(fresh, chosen, axis=0)]
    dynamic_update_slice x16 -> x0, local copies, waits for them, and re-layouts: 8.71 us -> none  [shards(): lax.map(one_document, (slot_queries.reshape((count, CAP) + slot_queries.s...]
  transfers between devices with their start and end apart: 6 -> 6, of which waited for: 6 -> 6; matrix products, arithmetic and copies ran while one was open for 6% -> 4% of each run, Pallas kernels for 0% -> 0%
where the time goes in v1:
time: 465 us; the launch traced here: 463 us
  waiting for transfers between devices  401 us (86%)
  Pallas kernels  28.7 us (6%)
  matrix products  13.6 us (3%)
  between operations  13.6 us (3%)
    all_gather x3, waiting for transfers between devices, project(): whole = lax.all_gather(weight, 'fsdp', axis=0, tiled=True)  206 us
    all_gather x1, waiting for transfers between devices, shards(): values = lax.all_gather(value_cache, 'fsdp', axis=0, tiled=True)  82.1 us
    all_gather x1, waiting for transfers between devices, shards(): keys = lax.all_gather(key_cache, 'fsdp', axis=0, tiled=True)  72.9 us
    all_gather x1, waiting for transfers between devices, shards(): full_rows = lax.all_gather(inputs, 'corpus', axis=1, tiled=True)  35.9 us
    pallas_call x1, Pallas kernels, attend(): pl.pallas_call(attend_kernel, out_shape=jax.ShapeDtypeStruct(q_lin.shape,...  28.7 us
    dot_general x3, matrix products, project(): return jnp.dot(normed, whole, preferred_element_type=jnp.float32)  13.6 us
  transfers between devices with their start and end apart: 6, of which 6 were waited for; matrix products, arithmetic and copies ran while one was open for 4% of the time, Pallas kernels for 0%

profile of v1, /device:TPU:0, one launch (start us, length us, event | category | flops | bytes accessed | tf_op | source)
XLA Modules:
  0.0 463.1 jit_solution(16774886290635042951)
XLA Ops:
  6.5 0.7 all-gather.7.cloned.1.call-update
  7.3 0.0 all-gather.13.cloned.1.call-start
  7.3 0.7 all-gather.13.cloned.1.call-update
  8.1 0.7 all-gather.11.cloned.1.call-update
  8.8 0.5 all-gather.9.cloned.1.call-update
  9.4 0.5 all-gather.15.cloned.1.call-update
  9.9 0.0 all-gather.17.cloned.1.call-start
  10.0 0.5 all-gather.17.cloned.1.call-update
  10.5 0.1 add_convert_fusion
  10.6 0.1 convert_element_type.19
  10.7 0.5 fusion.3
  11.2 0.1 pad_maximum_fusion
  11.4 35.9 %all-gather.7.cloned.1.call-done = bf16[256,4096]{1,0:T(8,128)(2,1)} async-done(((bf16[256,1024]{1,0:T(8,128)(2,1)}), bf16[256,4096]{1,0:T(8,128)(2,1)}) %all-gather.7.cloned.1.call-update) | async-done | bytes 2097168 | tf_op jit(solution)/shard_map/all_gather | solution.py:202
  47.3 2.2 fusion
  49.5 28.5 %all-gather.13.cloned.1.call-done = bf16[4096,256]{1,0:T(8,128)(2,1)} async-done(((bf16[512,256]{1,0:T(8,128)(2,1)}), bf16[4096,256]{1,0:T(8,128)(2,1)}) %all-gather.13.cloned.1.call-update) | async-done | bytes 2097168 | tf_op jit(solution)/shard_map/all_gather | solution.py:206
  78.0 2.4 fusion.4.v_ref
  80.4 27.8 %all-gather.11.cloned.1.call-done = bf16[4096,256]{1,0:T(8,128)(2,1)} async-done(((bf16[512,256]{1,0:T(8,128)(2,1)}), bf16[4096,256]{1,0:T(8,128)(2,1)}) %all-gather.11.cloned.1.call-update) | async-done | bytes 2097168 | tf_op jit(solution)/shard_map/all_gather | solution.py:206
  108.2 2.4 fusion.6.k_ref
  110.6 149.7 %all-gather.9.cloned.1.call-done = bf16[4096,2048]{1,0:T(8,128)(2,1)} async-done(((bf16[512,2048]{1,0:T(8,128)(2,1)}), bf16[4096,2048]{1,0:T(8,128)(2,1)}) %all-gather.9.cloned.1.call-update) | async-done | bytes 16777232 | tf_op jit(solution)/shard_map/all_gather | solution.py:206
  260.3 8.9 %fusion.8.q_ref = f32[256,2048]{1,0:T(8,128)S(1)} fusion(bf16[4096,2048]{1,0:T(8,128)(2,1)} %all-gather.9.cloned.1.call-done, bf16[256,4096]{1,0:T(8,128)(2,1)} %all-gather.7.cloned.1.call-done, f32[4096]{0:T(1024)S(1)} %copy-done.7, f32[256]{0:T(256)S(1)} %add_rsqrt_fusion), kind=kOutput, calls=%fused_computation.15 | convolution fusion | flops 4299161600 | bytes 20988928 | tf_op jit(solution)/shard_map/dot_general | solution.py:207
  269.2 72.9 %all-gather.15.cloned.1.call-done.keys_ref = bf16[8,2048,256]{2,1,0:T(8,128)(2,1)} async-done(((bf16[1,2048,256]{2,1,0:T(8,128)(2,1)}), bf16[8,2048,256]{2,1,0:T(8,128)(2,1)}) %all-gather.15.cloned.1.call-update) | async-done | bytes 8388624 | tf_op jit(solution)/shard_map/all_gather | solution.py:210
  342.1 82.1 %all-gather.17.cloned.1.call-done.values_ref = bf16[8,2048,256]{2,1,0:T(8,128)(2,1)} async-done(((bf16[1,2048,256]{2,1,0:T(8,128)(2,1)}), bf16[8,2048,256]{2,1,0:T(8,128)(2,1)}) %all-gather.17.cloned.1.call-update) | async-done | bytes 8388624 | tf_op jit(solution)/shard_map/all_gather | solution.py:211
  424.2 3.4 copy-done
  427.5 28.7 %shard_map.118 = bf16[256,2048]{1,0:T(8,128)(2,1)} custom-call(s32[4]{0:T(128)S(1)} %copy-done.5, s32[4]{0:T(128)S(1)} %copy-done.2, f32[256,2048]{1,0:T(8,128)S(1)} %fusion.8.q_ref, f32[256,256]{1,0:T(8,128)S(1)} %fusion.6.k_ref, f32[256,256]{1,0:T(8,128)S(1)} %fusion.4.v_ref, f32[1,2048]{1,0:T(1,128)S(1)} %bitcast.6, f32[1,256]{1,0:T(1,128)S(1)} %bitcast.7, ...), custom_call_target="tpu_custom_call" | custom-call | flops 4294967296 | bytes 16777216 | tf_op jit(solution)/shard_map/pallas_call | solution.py:152
  (21 shorter events, 0.2 us)
Async XLA Ops:
  6.5 40.7 %all-gather.7.cloned.1.call-start = ((), (), s32[]{:S(2)}) async-start(), calls=%async_computation | async-start | bytes 2621440 | tf_op jit(solution)/shard_map/all_gather | solution.py:202
  7.3 70.7 %all-gather.13.cloned.1.call-start = ((), (), s32[]{:S(2)}) async-start(), calls=%async_computation.3 | async-start | bytes 2359296 | tf_op jit(solution)/shard_map/all_gather | solution.py:206
  8.0 100.2 %all-gather.11.cloned.1.call-start = ((), (), s32[]{:S(2)}) async-start(), calls=%async_computation.2 | async-start | bytes 2359296 | tf_op jit(solution)/shard_map/all_gather | solution.py:206
  8.7 1.8 copy-start.2
  8.8 251.6 %all-gather.9.cloned.1.call-start = ((), (), s32[]{:S(2)}) async-start(), calls=%async_computation.1 | async-start | bytes 18874368 | tf_op jit(solution)/shard_map/all_gather | solution.py:206
  9.3 332.7 %all-gather.15.cloned.1.call-start = ((), (), s32[]{:S(2)}) async-start(), calls=%async_computation.4 | async-start | bytes 9437184 | tf_op jit(solution)/shard_map/all_gather | solution.py:210
  9.9 68.1 %copy-start.7 = (f32[4096]{0:T(1024)S(1)}, f32[4096]{0:T(1024)}, u32[]{:S(2)}) copy-start(f32[4096]{0:T(1024)} %param.13) | copy-start | bytes 49156
  9.9 414.2 %all-gather.17.cloned.1.call-start = ((), (), s32[]{:S(2)}) async-start(), calls=%async_computation.5 | async-start | bytes 9437184 | tf_op jit(solution)/shard_map/all_gather | solution.py:211
  47.3 30.7 %copy-start.6 = (bf16[256,4096]{1,0:T(8,128)(2,1)S(1)}, bf16[256,4096]{1,0:T(8,128)(2,1)}, u32[]{:S(2)}) copy-start(bf16[256,4096]{1,0:T(8,128)(2,1)} %all-gather.7.cloned.1.call-done) | copy-start | bytes 6291460
  110.6 313.5 %copy-start.1 = (f32[2048]{0:T(1024)S(1)}, f32[2048]{0:T(1024)}, u32[]{:S(2)}) copy-start(f32[2048]{0:T(1024)} %param.17) | copy-start | bytes 24580
  110.6 313.5 %copy-start.3 = (f32[256]{0:T(256)S(1)}, f32[256]{0:T(256)}, u32[]{:S(2)}) copy-start(f32[256]{0:T(256)} %param.18) | copy-start | bytes 3076
  110.6 313.5 %copy-start.4 = (f32[256]{0:T(256)S(1)}, f32[256]{0:T(256)}, u32[]{:S(2)}) copy-start(f32[256]{0:T(256)} %param.19) | copy-start | bytes 3076
  110.6 313.5 %copy-start.5 = (s32[4]{0:T(128)S(1)}, s32[4]{0:T(128)}, u32[]{:S(2)}) copy-start(s32[4]{0:T(128)} %doc_ref.1) | copy-start | bytes 52
  424.2 3.4 copy-start
Sparse Core Ops, SparseCore 0:
  9.2 38.0 all-gather.6
  48.8 29.0 all-gather.12
  79.6 28.5 all-gather.10
  109.7 150.5 all-gather.8
  261.7 80.2 all-gather.14
  343.5 80.5 all-gather.16

commit v2 on v1

--- a/solution.py
+++ b/solution.py
@@ -11,6 +11,7 @@
 THETA = 1000000.0
 MASKED = -1e30
 KEY_BLOCK = 512
+SENT = jnp.float32
 
 
 def rope_tables(position, width):
@@ -185,7 +186,7 @@
     )(source_doc, prefix_len, q_lin, k_lin, v_lin, q_bias[None], k_bias[None], v_bias[None], cosine, sine, keys, values)
 
 
-def shards(
+def gather_all(
     inputs,
     norm_gain,
     w_query,
@@ -216,6 +217,134 @@
     )
 
 
+def swap_cores(array):
+    count = lax.axis_size("fsdp")
+    return lax.ppermute(array, "fsdp", [(f, f ^ 1) for f in range(count)])
+
+
+def in_core_order(mine, other, core):
+    return jnp.where(core == 0, jnp.stack([mine, other]), jnp.stack([other, mine]))
+
+
+def half_of(array, which, axis=1):
+    size = array.shape[axis] // 2
+    return lax.dynamic_slice_in_dim(array, which * size, size, axis)
+
+
+def along_line(array, step):
+    count = lax.axis_size("fsdp")
+    held, parts = array, []
+    for hop in range(1, count // 2):
+        if step > 0:
+            sources = range(2 * (hop - 1), count - 2)
+        else:
+            sources = range(2, count - 2 * (hop - 1))
+        held = lax.ppermute(held, "fsdp", [(f, f + 2 * step) for f in sources])
+        parts.append(held)
+    return parts
+
+
+def split_heads(
+    inputs,
+    norm_gain,
+    w_query,
+    w_key,
+    w_value,
+    query_bias,
+    key_bias,
+    value_bias,
+    key_cache,
+    value_cache,
+    source_doc,
+    prefix_len,
+):
+    count = lax.axis_size("fsdp")
+    lines = count // 2
+    index = lax.axis_index("fsdp")
+    core = lax.rem(index, 2)
+    line = lax.div(index, 2)
+    tokens = inputs.shape[0]
+
+    def cache_table(cache):
+        pair = in_core_order(half_of(cache[0], core), swap_cores(half_of(cache[0], 1 - core)), core)
+        return jnp.concatenate([pair] + along_line(pair, 1) + along_line(pair, -1))
+
+    keys = cache_table(key_cache)
+    values = cache_table(value_cache)
+
+    mine = jnp.concatenate([half_of(w, core) for w in (w_query, w_key, w_value)], axis=1)
+    other = swap_cores(
+        jnp.concatenate([half_of(w, 1 - core) for w in (w_query, w_key, w_value)], axis=1)
+    )
+    weight = in_core_order(mine, other, core).reshape(2 * mine.shape[0], mine.shape[1])
+
+    full_rows = lax.all_gather(inputs, "corpus", axis=1, tiled=True)
+    normed = normalize(full_rows, norm_gain)
+    wide = normed.shape[1] // lines
+    by_line = normed.reshape(tokens, lines, wide)
+    pieces = [lax.dynamic_index_in_dim(by_line, line, 1, keepdims=False)]
+    for shift in range(1, lines):
+        sent = lax.dynamic_index_in_dim(by_line, lax.rem(line + shift, lines), 1, keepdims=False)
+        pairs = [(f, (f + 2 * shift) % count) for f in range(count)]
+        pieces.append(lax.ppermute(sent, "fsdp", pairs))
+    block = jnp.stack(pieces)
+    both = in_core_order(block, swap_cores(block), core)
+    both = jnp.swapaxes(both, 0, 1)
+    partial = jnp.einsum("zctd,dn->zctn", both, weight, preferred_element_type=jnp.float32)
+    at = lax.rem(line - jnp.arange(lines) + lines, lines)
+    partial = jnp.concatenate(
+        [lax.dynamic_index_in_dim(partial, at[z], 0) for z in range(lines)]
+    ).astype(SENT)
+    groups = [[2 * z + c for z in range(lines)] for c in range(2)]
+    lin = lax.psum_scatter(
+        partial.reshape(count * tokens, -1),
+        "fsdp",
+        scatter_dimension=0,
+        axis_index_groups=groups,
+        tiled=True,
+    ).astype(jnp.float32)
+    heads = query_bias.shape[0] // 2
+    q_lin = lin[:, :heads]
+    k_lin = lin[:, heads : heads + HD]
+    v_lin = lin[:, heads + HD :]
+
+    facts = jnp.stack([source_doc, prefix_len])
+    facts = jnp.swapaxes(in_core_order(facts, swap_cores(facts), core), 0, 1).reshape(2, -1)
+    docs, lengths = facts[0], facts[1]
+    away = line - lax.div(docs, 2)
+    slot = 2 * jnp.where(away >= 0, away, lines - 1 - away) + lax.rem(docs, 2)
+    position = lengths[:, None] + jnp.arange(SL, dtype=jnp.int32)[None, :]
+    cosine, sine = rope_tables(position.reshape(-1), HD)
+    out = attend(
+        slot,
+        lengths,
+        q_lin,
+        k_lin,
+        v_lin,
+        half_of(query_bias, core, 0),
+        half_of(key_bias, core, 0),
+        half_of(value_bias, core, 0),
+        cosine,
+        sine,
+        keys,
+        values,
+    )
+    kept = half_of(out, core, 0)
+    got = swap_cores(half_of(out, 1 - core, 0))
+    return jnp.where(
+        core == 0,
+        jnp.concatenate([kept, got], axis=1),
+        jnp.concatenate([got, kept], axis=1),
+    )
+
+
+def shards(*arrays):
+    lines = lax.axis_size("fsdp") // 2
+    if arrays[3].shape[1] == 2 * HD and lines == 4:
+        return split_heads(*arrays)
+    return gather_all(*arrays)
+
+
 def solution(mesh):
     in_specs = (
         P("fsdp", "corpus"),

time: 465 us -> 499 us (1.073)
  waiting for transfers between devices: 401 us -> 353 us
  local copies, waits for them, and re-layouts: 3.5 us -> 37.4 us
  starting transfers between devices: 0.19 us -> 25.8 us
  other arithmetic: 3 us -> 23.7 us
  between operations: 13.6 us -> 21.3 us
  matrix products: 13.6 us -> 8.11 us
    all_gather x6 -> x1, waiting for transfers between devices: 397 us -> 38.5 us  [split_heads(): full_rows = lax.all_gather(inputs, 'corpus', axis=1, tiled=True)]
    ppermute x0 -> x21, waiting for transfers between devices: none -> 315 us  [the longest x12 272 us: along_line(): held = lax.ppermute(held, 'fsdp', [(f, f + 2 * step) for f in sources])]
    ppermute x0 -> x21, starting transfers between devices: none -> 25.7 us  [the longest x12 20.4 us: along_line(): held = lax.ppermute(held, 'fsdp', [(f, f + 2 * step) for f in sources])]
    unnamed x16 -> x37, local copies, waits for them, and re-layouts: 3.41 us -> 21.8 us
    dynamic_slice x0 -> x12, local copies, waits for them, and re-layouts: none -> 9.56 us  [the longest x1 3.47 us: split_heads(): lax.dynamic_index_in_dim(partial, at[z], 0)]
    concatenate x0 -> x2, other arithmetic: none -> 7.86 us  [the longest x1 7.76 us: split_heads(): jnp.concatenate([lax.dynamic_index_in_dim(partial, at[z], 0) for z in ran...]
    dot_general x3 -> x1, matrix products: 13.6 us -> 8.11 us  [split_heads(): jnp.einsum('zctd,dn->zctn', both, weight, preferred_element_type=jnp.floa...]
  transfers between devices with their start and end apart: 6 -> 23, of which waited for: 6 -> 12; matrix products, arithmetic and copies ran while one was open for 4% -> 6% of each run, Pallas kernels for 0% -> 0%
where the time goes in v2:
time: 499 us; the launch traced here: 500 us
  waiting for transfers between devices  353 us (71%)
  local copies, waits for them, and re-layouts  37.4 us (7%)
  Pallas kernels  30 us (6%)
  starting transfers between devices  25.8 us (5%)
  other arithmetic  23.7 us (5%)
  between operations  21.3 us (4%)
  matrix products  8.11 us (2%)
    ppermute x12, waiting for transfers between devices, along_line(): held = lax.ppermute(held, 'fsdp', [(f, f + 2 * step) for f in sources])  272 us
    ppermute x3, waiting for transfers between devices, split_heads(): pieces.append(lax.ppermute(sent, 'fsdp', pairs))  40.2 us
    all_gather x1, waiting for transfers between devices, split_heads(): full_rows = lax.all_gather(inputs, 'corpus', axis=1, tiled=True)  38.5 us
    pallas_call x1, Pallas kernels, attend(): pl.pallas_call(attend_kernel, out_shape=jax.ShapeDtypeStruct(q_lin.shape,...  30 us
    unnamed x37, local copies, waits for them, and re-layouts  21.8 us
    ppermute x12, starting transfers between devices, along_line(): held = lax.ppermute(held, 'fsdp', [(f, f + 2 * step) for f in sources])  20.4 us
  transfers between devices with their start and end apart: 23, of which 12 were waited for; matrix products, arithmetic and copies ran while one was open for 6% of the time, Pallas kernels for 0%

profile of v2, /device:TPU:0, one launch (start us, length us, event | category | flops | bytes accessed | tf_op | source)
XLA Modules:
  0.0 499.8 jit_solution(12856538802882183907)
XLA Ops:
  8.7 38.5 %all-gather.2.cloned.1.call-done = bf16[256,4096]{0,1:T(8,128)(2,1)} async-done(((bf16[256,1024]{0,1:T(8,128)(2,1)}), bf16[256,4096]{0,1:T(8,128)(2,1)}) %all-gather.2.cloned.1.call-update) | async-done | bytes 2097168 | tf_op jit(solution)/shard_map/all_gather | solution.py:281
  47.3 2.3 fusion
  51.5 3.3 collective-permute-start.3
  59.9 7.7 %collective-permute-done.3 = bf16[256,1024]{1,0:T(8,128)(2,1)} collective-permute-done((bf16[256,1024]{1,0:T(8,128)(2,1)}, bf16[256,1024]{1,0:T(8,128)(2,1)}, u32[]{:S(2)}, u32[]{:S(2)}) %collective-permute-start.3) | collective-permute-done | bytes 524320 | tf_op jit(solution)/shard_map/ppermute | solution.py:289
  67.5 32.5 %collective-permute-done.2 = bf16[256,1024]{1,0:T(8,128)(2,1)} collective-permute-done((bf16[256,1024]{1,0:T(8,128)(2,1)}, bf16[256,1024]{1,0:T(8,128)(2,1)}, u32[]{:S(2)}, u32[]{:S(2)}) %collective-permute-start.2) | collective-permute-done | bytes 524320 | tf_op jit(solution)/shard_map/ppermute | solution.py:289
  100.1 3.8 fusion.12
  114.5 2.2 maximum_select_fusion.1
  116.8 8.1 %fusion.4 = f32[4,2,256,1280]{3,2,1,0:T(8,128)S(1)} fusion(bf16[1024,1280,1,1]{1,0,3,2:T(8,128)(2,1)S(1)} %bitcast.50, bf16[1,4,256,1024]{3,2,1,0:T(8,128)(2,1)} %bitcast.14, bf16[1,4,256,1024]{3,2,1,0:T(8,128)(2,1)S(1)} %copy-done.2, pred[]{:T(512)S(6)} %eq.2), kind=kOutput, calls=%fused_computation.8 | convolution fusion | flops 5375000576 | bytes 17301504 | tf_op jit(solution)/shard_map/zctd,dn->zctn/dot_general | solution.py:293
  125.0 3.5 constant_dynamic-slice_fusion.7
  128.4 7.8 %pad_maximum_fusion = f32[4,2,256,1280]{3,2,1,0:T(8,128)} fusion(f32[1,2,256,1280]{3,2,1,0:T(8,128)} %get-tuple-element.12, f32[1,2,256,1280]{3,2,1,0:T(8,128)} %get-tuple-element.13, f32[1,2,256,1280]{3,2,1,0:T(8,128)} %get-tuple-element.14, f32[1,2,256,1280]{3,2,1,0:T(8,128)S(1)} %get-tuple-element.11), kind=kLoop, calls=%fused_computation | loop fusion | flops 7864320 | bytes 20971520 | tf_op jit(solution)/shard_map/concatenate | solution.py:295
  141.1 4.4 collective-permute-start.7
  147.0 4.3 collective-permute-start.14
  154.2 36.4 %collective-permute-done.7 = bf16[2,2048,128]{2,1,0:T(8,128)(2,1)} collective-permute-done((bf16[2,2048,128]{2,1,0:T(8,128)(2,1)}, bf16[2,2048,128]{2,1,0:T(8,128)(2,1)}, u32[]{:S(2)}, u32[]{:S(2)}) %collective-permute-start.7) | collective-permute-done | bytes 1048608 | tf_op jit(solution)/shard_map/ppermute | solution.py:242
  192.8 42.5 %collective-permute-done.14 = bf16[2,2048,128]{2,1,0:T(8,128)(2,1)} collective-permute-done((bf16[2,2048,128]{2,1,0:T(8,128)(2,1)}, bf16[2,2048,128]{2,1,0:T(8,128)(2,1)}, u32[]{:S(2)}, u32[]{:S(2)}) %collective-permute-start.14) | collective-permute-done | bytes 1048608 | tf_op jit(solution)/shard_map/ppermute | solution.py:242
  238.4 49.8 %collective-permute-done.17 = bf16[2,2048,128]{2,1,0:T(8,128)(2,1)S(1)} collective-permute-done((bf16[2,2048,128]{2,1,0:T(8,128)(2,1)}, bf16[2,2048,128]{2,1,0:T(8,128)(2,1)S(1)}, u32[]{:S(2)}, u32[]{:S(2)}) %collective-permute-start.17) | collective-permute-done | bytes 1048608 | tf_op jit(solution)/shard_map/ppermute | solution.py:242
  290.4 2.3 constant_dynamic-update-slice_fusion.5
  292.7 2.3 constant_dynamic-update-slice_fusion.12
  295.7 2.3 constant_dynamic-update-slice_fusion.4
  298.0 68.4 %collective-permute-done.11 = bf16[2,2048,128]{2,1,0:T(8,128)(2,1)S(1)} collective-permute-done((bf16[2,2048,128]{2,1,0:T(8,128)(2,1)S(1)}, bf16[2,2048,128]{2,1,0:T(8,128)(2,1)S(1)}, u32[]{:S(2)}, u32[]{:S(2)}) %collective-permute-start.11) | collective-permute-done | bytes 1048608 | tf_op jit(solution)/shard_map/ppermute | solution.py:242
  367.7 35.1 %collective-permute-done.18 = bf16[2,2048,128]{2,1,0:T(8,128)(2,1)S(1)} collective-permute-done((bf16[2,2048,128]{2,1,0:T(8,128)(2,1)S(1)}, bf16[2,2048,128]{2,1,0:T(8,128)(2,1)S(1)}, u32[]{:S(2)}, u32[]{:S(2)}) %collective-permute-start.18) | collective-permute-done | bytes 1048608 | tf_op jit(solution)/shard_map/ppermute | solution.py:242
  411.5 19.2 %collective-permute-done.12 = bf16[2,2048,128]{2,1,0:T(8,128)(2,1)S(1)} collective-permute-done((bf16[2,2048,128]{2,1,0:T(8,128)(2,1)S(1)}, bf16[2,2048,128]{2,1,0:T(8,128)(2,1)S(1)}, u32[]{:S(2)}, u32[]{:S(2)}) %collective-permute-start.12) | collective-permute-done | bytes 1048608 | tf_op jit(solution)/shard_map/ppermute | solution.py:242
  431.7 20.7 %collective-permute-done.19 = bf16[2,2048,128]{2,1,0:T(8,128)(2,1)S(1)} collective-permute-done((bf16[2,2048,128]{2,1,0:T(8,128)(2,1)S(1)}, bf16[2,2048,128]{2,1,0:T(8,128)(2,1)S(1)}, u32[]{:S(2)}, u32[]{:S(2)}) %collective-permute-start.19) | collective-permute-done | bytes 1048608 | tf_op jit(solution)/shard_map/ppermute | solution.py:242
  456.4 3.1 copy-done
  459.5 30.0 %shard_map.118 = bf16[512,1024]{1,0:T(8,128)(2,1)S(1)} custom-call(s32[8]{0:T(128)S(1)} %fusion.8.doc_ref, s32[8]{0:T(128)S(1)} %squeeze.37.len_ref, f32[512,1024]{1,0:T(8,128)S(1)} %slice.40.q_ref, f32[512,128]{1,0:T(8,128)S(1)} %get-tuple-element.16.k_ref, f32[512,128]{1,0:T(8,128)S(1)} %get-tuple-element.15.v_ref, f32[1,1024]{1,0:T(1,128)S(1)} %bitcast.47, ...), custom_call_target="tpu_custom_call" | custom-call | flops 4294967296 | bytes 16777216 | tf_op jit(solution)/shard_map/pallas_call | solution.py:153
  (104 shorter events, 48.1 us)
Async XLA Ops:
  6.5 40.7 %all-gather.2.cloned.1.call-start = ((), (), s32[]{:S(2)}) async-start(), calls=%async_computation.1 | async-start | bytes 2621440 | tf_op jit(solution)/shard_map/all_gather | solution.py:281
  8.6 444.9 %reduce-scatter.2.cloned.1.call-start = ((), (), s32[]{:S(2)}) async-start(), calls=%async_computation.2 | async-start | bytes 13107200 | tf_op jit(solution)/shard_map/reduce_scatter | solution.py:299
  51.5 16.1 %collective-permute-start.3 = (bf16[256,1024]{1,0:T(8,128)(2,1)}, bf16[256,1024]{1,0:T(8,128)(2,1)}, u32[]{:S(2)}, u32[]{:S(2)}) collective-permute-start(bf16[256,1024]{1,0:T(8,128)(2,1)} %bitcast.11), channel_id=1, source_target_pairs={{0,6},{1,7},{2,0},{3,1},{4,2},{5,3},{6,4},{7,5},{8,14},{9,15},{10,... | collective-permute-start | bytes 1572872 | tf_op jit(solution)/shard_map/ppermute | solution.py:289
  55.8 44.3 %collective-permute-start.2 = (bf16[256,1024]{1,0:T(8,128)(2,1)}, bf16[256,1024]{1,0:T(8,128)(2,1)}, u32[]{:S(2)}, u32[]{:S(2)}) collective-permute-start(bf16[256,1024]{1,0:T(8,128)(2,1)} %bitcast.9), channel_id=1, source_target_pairs={{0,4},{1,5},{2,6},{3,7},{4,0},{5,1},{6,2},{7,3},{8,12},{9,13},{10,... | collective-permute-start | bytes 1572872 | tf_op jit(solution)/shard_map/ppermute | solution.py:289
  56.8 43.2 %collective-permute-start.1 = (bf16[256,1024]{1,0:T(8,128)(2,1)}, bf16[256,1024]{1,0:T(8,128)(2,1)}, u32[]{:S(2)}, u32[]{:S(2)}) collective-permute-start(bf16[256,1024]{1,0:T(8,128)(2,1)} %bitcast.7), channel_id=1, source_target_pairs={{0,2},{1,3},{2,4},{3,5},{4,6},{5,7},{6,0},{7,1},{8,10},{9,11},{10,... | collective-permute-start | bytes 1572872 | tf_op jit(solution)/shard_map/ppermute | solution.py:289
  103.9 12.8 %collective-permute-start.4 = (bf16[4,256,1024]{2,1,0:T(8,128)(2,1)}, bf16[4,256,1024]{2,1,0:T(8,128)(2,1)}, u32[]{:S(2)}, u32[]{:S(2)}) collective-permute-start(bf16[4,256,1024]{2,1,0:T(8,128)(2,1)} %get-tuple-element.18), channel_id=1, source_target_pairs={{0,1},{1,0},{2,3},{3,2},{4,5},{5,4},{6,7},{7,6},{8,9},{9,8},{10,11... | collective-permute-start | bytes 6291464 | tf_op jit(solution)/shard_map/ppermute | solution.py:222
  104.7 9.7 %collective-permute-start.5 = (bf16[512,1280]{1,0:T(8,128)(2,1)S(1)}, bf16[512,1280]{1,0:T(8,128)(2,1)}, u32[]{:S(2)}, u32[]{:S(2)}) collective-permute-start(bf16[512,1280]{1,0:T(8,128)(2,1)S(1)} %pad_maximum_fusion.2), channel_id=1, source_target_pairs={{0,1},{1,0},{2,3},{3,2},{4,5},{5,4},{6,7},{7,6},{8,9},{9,8},{10,11... | collective-permute-start | bytes 3932168 | tf_op jit(solution)/shard_map/ppermute | solution.py:222
  137.5 2.0 collective-permute-start.6
  138.7 6.8 %collective-permute-start.13 = (bf16[2048,128]{1,0:T(8,128)(2,1)S(1)}, bf16[2048,128]{1,0:T(8,128)(2,1)S(1)}, u32[]{:S(2)}, u32[]{:S(2)}) collective-permute-start(bf16[2048,128]{1,0:T(8,128)(2,1)S(1)} %get-tuple-element.27), channel_id=1, source_target_pairs={{0,1},{1,0},{2,3},{3,2},{4,5},{5,4},{6,7},{7,6},{8,9},{9,8},{10,11... | collective-permute-start | bytes 1572872 | tf_op jit(solution)/shard_map/ppermute | solution.py:222
  139.5 52.9 %copy-start.12 = (f32[256]{0:T(256)S(1)}, f32[256]{0:T(256)}, u32[]{:S(2)}) copy-start(f32[256]{0:T(256)} %param.18) | copy-start | bytes 3076
  141.1 49.6 %collective-permute-start.7 = (bf16[2,2048,128]{2,1,0:T(8,128)(2,1)}, bf16[2,2048,128]{2,1,0:T(8,128)(2,1)}, u32[]{:S(2)}, u32[]{:S(2)}) collective-permute-start(bf16[2,2048,128]{2,1,0:T(8,128)(2,1)} %get-tuple-element.10), channel_id=1, source_target_pairs={{0,2},{1,3},{2,4},{3,5},{4,6},{5,7},{8,10},{9,11},{10,12},{11,13},... | collective-permute-start | bytes 3145736 | tf_op jit(solution)/shard_map/ppermute | solution.py:242
  147.0 88.3 %collective-permute-start.14 = (bf16[2,2048,128]{2,1,0:T(8,128)(2,1)}, bf16[2,2048,128]{2,1,0:T(8,128)(2,1)}, u32[]{:S(2)}, u32[]{:S(2)}) collective-permute-start(bf16[2,2048,128]{2,1,0:T(8,128)(2,1)} %get-tuple-element.8), channel_id=1, source_target_pairs={{0,2},{1,3},{2,4},{3,5},{4,6},{5,7},{8,10},{9,11},{10,12},{11,13},... | collective-permute-start | bytes 3145736 | tf_op jit(solution)/shard_map/ppermute | solution.py:242
  151.4 85.7 %collective-permute-start.10 = (bf16[2,2048,128]{2,1,0:T(8,128)(2,1)}, bf16[2,2048,128]{2,1,0:T(8,128)(2,1)S(1)}, u32[]{:S(2)}, u32[]{:S(2)}) collective-permute-start(bf16[2,2048,128]{2,1,0:T(8,128)(2,1)} %get-tuple-element.10), channel_id=1, source_target_pairs={{2,0},{3,1},{4,2},{5,3},{6,4},{7,5},{10,8},{11,9},{12,10},{13,11},... | collective-permute-start | bytes 3145736 | tf_op jit(solution)/shard_map/ppermute | solution.py:242
  152.7 135.5 %collective-permute-start.17 = (bf16[2,2048,128]{2,1,0:T(8,128)(2,1)}, bf16[2,2048,128]{2,1,0:T(8,128)(2,1)S(1)}, u32[]{:S(2)}, u32[]{:S(2)}) collective-permute-start(bf16[2,2048,128]{2,1,0:T(8,128)(2,1)} %get-tuple-element.8), channel_id=1, source_target_pairs={{2,0},{3,1},{4,2},{5,3},{6,4},{7,5},{10,8},{11,9},{12,10},{13,11},... | collective-permute-start | bytes 3145736 | tf_op jit(solution)/shard_map/ppermute | solution.py:242
  154.2 38.3 %collective-permute-start = (s32[2,4]{1,0:T(2,128)S(1)}, s32[2,4]{1,0:T(2,128)S(1)}, u32[]{:S(2)}, u32[]{:S(2)}) collective-permute-start(s32[2,4]{1,0:T(2,128)S(1)} %get-tuple-element.39), channel_id=1, source_target_pairs={{0,1},{1,0},{2,3},{3,2},{4,5},{5,4},{6,7},{7,6},{8,9},{9,8},{10,11... | collective-permute-start | bytes 104 | tf_op jit(solution)/shard_map/ppermute | solution.py:222
  190.7 98.8 %collective-permute-start.8 = (bf16[2,2048,128]{2,1,0:T(8,128)(2,1)}, bf16[2,2048,128]{2,1,0:T(8,128)(2,1)}, u32[]{:S(2)}, u32[]{:S(2)}) collective-permute-start(bf16[2,2048,128]{2,1,0:T(8,128)(2,1)} %collective-permute-done.7), channel_id=1, source_target_pairs={{2,4},{3,5},{4,6},{5,7},{10,12},{11,13},{12,14},{13,15},{18,20},{1... | collective-permute-start | bytes 3145736 | tf_op jit(solution)/shard_map/ppermute | solution.py:242
  235.4 59.6 %collective-permute-start.15 = (bf16[2,2048,128]{2,1,0:T(8,128)(2,1)}, bf16[2,2048,128]{2,1,0:T(8,128)(2,1)S(1)}, u32[]{:S(2)}, u32[]{:S(2)}) collective-permute-start(bf16[2,2048,128]{2,1,0:T(8,128)(2,1)} %collective-permute-done.14), channel_id=1, source_target_pairs={{2,4},{3,5},{4,6},{5,7},{10,12},{11,13},{12,14},{13,15},{18,20},{1... | collective-permute-start | bytes 3145736 | tf_op jit(solution)/shard_map/ppermute | solution.py:242
  237.1 129.3 %collective-permute-start.11 = (bf16[2,2048,128]{2,1,0:T(8,128)(2,1)S(1)}, bf16[2,2048,128]{2,1,0:T(8,128)(2,1)S(1)}, u32[]{:S(2)}, u32[]{:S(2)}) collective-permute-start(bf16[2,2048,128]{2,1,0:T(8,128)(2,1)S(1)} %collective-permute-done.10), channel_id=1, source_target_pairs={{2,0},{3,1},{4,2},{5,3},{10,8},{11,9},{12,10},{13,11},{18,16},{19,... | collective-permute-start | bytes 3145736 | tf_op jit(solution)/shard_map/ppermute | solution.py:242
  288.1 114.6 %collective-permute-start.18 = (bf16[2,2048,128]{2,1,0:T(8,128)(2,1)S(1)}, bf16[2,2048,128]{2,1,0:T(8,128)(2,1)S(1)}, u32[]{:S(2)}, u32[]{:S(2)}) collective-permute-start(bf16[2,2048,128]{2,1,0:T(8,128)(2,1)S(1)} %collective-permute-done.17), channel_id=1, source_target_pairs={{2,0},{3,1},{4,2},{5,3},{10,8},{11,9},{12,10},{13,11},{18,16},{19,... | collective-permute-start | bytes 3145736 | tf_op jit(solution)/shard_map/ppermute | solution.py:242
  289.5 115.7 %collective-permute-start.9 = (bf16[2,2048,128]{2,1,0:T(8,128)(2,1)}, bf16[2,2048,128]{2,1,0:T(8,128)(2,1)S(1)}, u32[]{:S(2)}, u32[]{:S(2)}) collective-permute-start(bf16[2,2048,128]{2,1,0:T(8,128)(2,1)} %collective-permute-done.8), channel_id=1, source_target_pairs={{4,6},{5,7},{12,14},{13,15},{20,22},{21,23},{28,30},{29,31}} | collective-permute-start | bytes 3145736 | tf_op jit(solution)/shard_map/ppermute | solution.py:242
  295.0 113.3 %collective-permute-start.16 = (bf16[2,2048,128]{2,1,0:T(8,128)(2,1)S(1)}, bf16[2,2048,128]{2,1,0:T(8,128)(2,1)S(1)}, u32[]{:S(2)}, u32[]{:S(2)}) collective-permute-start(bf16[2,2048,128]{2,1,0:T(8,128)(2,1)S(1)} %collective-permute-done.15), channel_id=1, source_target_pairs={{4,6},{5,7},{12,14},{13,15},{20,22},{21,23},{28,30},{29,31}} | collective-permute-start | bytes 3145736 | tf_op jit(solution)/shard_map/ppermute | solution.py:242
  366.4 64.3 %collective-permute-start.12 = (bf16[2,2048,128]{2,1,0:T(8,128)(2,1)S(1)}, bf16[2,2048,128]{2,1,0:T(8,128)(2,1)S(1)}, u32[]{:S(2)}, u32[]{:S(2)}) collective-permute-start(bf16[2,2048,128]{2,1,0:T(8,128)(2,1)S(1)} %collective-permute-done.11), channel_id=1, source_target_pairs={{2,0},{3,1},{10,8},{11,9},{18,16},{19,17},{26,24},{27,25}} | collective-permute-start | bytes 3145736 | tf_op jit(solution)/shard_map/ppermute | solution.py:242
  402.8 49.6 %collective-permute-start.19 = (bf16[2,2048,128]{2,1,0:T(8,128)(2,1)S(1)}, bf16[2,2048,128]{2,1,0:T(8,128)(2,1)S(1)}, u32[]{:S(2)}, u32[]{:S(2)}) collective-permute-start(bf16[2,2048,128]{2,1,0:T(8,128)(2,1)S(1)} %collective-permute-done.18), channel_id=1, source_target_pairs={{2,0},{3,1},{10,8},{11,9},{18,16},{19,17},{26,24},{27,25}} | collective-permute-start | bytes 3145736 | tf_op jit(solution)/shard_map/ppermute | solution.py:242
  489.6 2.0 collective-permute-start.20
  (12 other events, 196.0 us)
Sparse Core Ops, SparseCore 0:
  9.2 38.0 all-gather.1
  136.3 256.4 reduce-scatter.1

commit v3 on v2

--- a/solution.py
+++ b/solution.py
@@ -231,17 +231,17 @@
     return lax.dynamic_slice_in_dim(array, which * size, size, axis)
 
 
-def along_line(array, step):
+def one_hop(array, hop, step):
     count = lax.axis_size("fsdp")
-    held, parts = array, []
-    for hop in range(1, count // 2):
-        if step > 0:
-            sources = range(2 * (hop - 1), count - 2)
-        else:
-            sources = range(2, count - 2 * (hop - 1))
-        held = lax.ppermute(held, "fsdp", [(f, f + 2 * step) for f in sources])
-        parts.append(held)
-    return parts
+    if step > 0:
+        sources = range(2 * (hop - 1), count - 2)
+    else:
+        sources = range(2, count - 2 * (hop - 1))
+    return lax.ppermute(array, "fsdp", [(f, f + 2 * step) for f in sources])
+
+
+def hop_both(held, hop):
+    return [one_hop(array, hop, step) for array, step in zip(held, (1, -1, 1, -1))]
 
 
 def split_heads(
@@ -265,12 +265,11 @@
     line = lax.div(index, 2)
     tokens = inputs.shape[0]
 
-    def cache_table(cache):
-        pair = in_core_order(half_of(cache[0], core), swap_cores(half_of(cache[0], 1 - core)), core)
-        return jnp.concatenate([pair] + along_line(pair, 1) + along_line(pair, -1))
-
-    keys = cache_table(key_cache)
-    values = cache_table(value_cache)
+    def pair_of(cache):
+        return in_core_order(half_of(cache[0], core), swap_cores(half_of(cache[0], 1 - core)), core)
+
+    own_k, own_v = pair_of(key_cache), pair_of(value_cache)
+    hop1 = hop_both([own_k, own_k, own_v, own_v], 1)
 
     mine = jnp.concatenate([half_of(w, core) for w in (w_query, w_key, w_value)], axis=1)
     other = swap_cores(
@@ -280,6 +279,8 @@
 
     full_rows = lax.all_gather(inputs, "corpus", axis=1, tiled=True)
     normed = normalize(full_rows, norm_gain)
+    normed, weight, hop1 = lax.optimization_barrier((normed, weight, hop1))
+    hop2 = hop_both(hop1, 2)
     wide = normed.shape[1] // lines
     by_line = normed.reshape(tokens, lines, wide)
     pieces = [lax.dynamic_index_in_dim(by_line, line, 1, keepdims=False)]
@@ -290,19 +291,21 @@
     block = jnp.stack(pieces)
     both = in_core_order(block, swap_cores(block), core)
     both = jnp.swapaxes(both, 0, 1)
-    partial = jnp.einsum("zctd,dn->zctn", both, weight, preferred_element_type=jnp.float32)
     at = lax.rem(line - jnp.arange(lines) + lines, lines)
-    partial = jnp.concatenate(
-        [lax.dynamic_index_in_dim(partial, at[z], 0) for z in range(lines)]
-    ).astype(SENT)
+    both = jnp.concatenate([lax.dynamic_index_in_dim(both, at[z], 0) for z in range(lines)])
+    both, hop2 = lax.optimization_barrier((both.reshape(count * tokens, -1), hop2))
+    hop3 = hop_both(hop2, 3)
+    partial = jnp.dot(both, weight, preferred_element_type=jnp.float32).astype(SENT)
     groups = [[2 * z + c for z in range(lines)] for c in range(2)]
     lin = lax.psum_scatter(
-        partial.reshape(count * tokens, -1),
+        partial,
         "fsdp",
         scatter_dimension=0,
         axis_index_groups=groups,
         tiled=True,
     ).astype(jnp.float32)
+    keys = jnp.concatenate([own_k] + [hop[i] for i in (0, 1) for hop in (hop1, hop2, hop3)])
+    values = jnp.concatenate([own_v] + [hop[i] for i in (2, 3) for hop in (hop1, hop2, hop3)])
     heads = query_bias.shape[0] // 2
     q_lin = lin[:, :heads]
     k_lin = lin[:, heads : heads + HD]

time: 499 us -> 452 us (0.906)
  waiting for transfers between devices: 353 us -> 302 us
  starting transfers between devices: 25.8 us -> 32.6 us
    ppermute x12, waiting for transfers between devices: 272 us -> 195 us  [one_hop(): return lax.ppermute(array, 'fsdp', [(f, f + 2 * step) for f in sources])]
    reduce_scatter x1, waiting for transfers between devices: 0.01 us -> 62.4 us  [split_heads(): lax.psum_scatter(partial, 'fsdp', scatter_dimension=0, axis_index_groups=...]
    all_gather x1, waiting for transfers between devices: 38.5 us -> 8.69 us  [split_heads(): full_rows = lax.all_gather(inputs, 'corpus', axis=1, tiled=True)]
    ppermute x3, waiting for transfers between devices: 40.2 us -> 32.6 us  [split_heads(): pieces.append(lax.ppermute(sent, 'fsdp', pairs))]
    concatenate x1, other arithmetic: 7.76 us -> 0.57 us  [split_heads(): jnp.concatenate([lax.dynamic_index_in_dim(both, at[z], 0) for z in range(...]
    unnamed x37 -> x39, local copies, waits for them, and re-layouts: 21.8 us -> 26.5 us
  transfers between devices with their start and end apart: 23 -> 23, of which waited for: 12 -> 13; matrix products, arithmetic and copies ran while one was open for 6% -> 10% of each run, Pallas kernels for 0% -> 0%
where the time goes in v3:
time: 452 us; the launch traced here: 450 us
  waiting for transfers between devices  302 us (67%)
  local copies, waits for them, and re-layouts  39.4 us (9%)
  starting transfers between devices  32.6 us (7%)
  Pallas kernels  25.6 us (6%)
  other arithmetic  21.9 us (5%)
  between operations  20.9 us (5%)
  matrix products  8.12 us (2%)
    ppermute x12, waiting for transfers between devices, one_hop(): return lax.ppermute(array, 'fsdp', [(f, f + 2 * step) for f in sources])  195 us
    reduce_scatter x1, waiting for transfers between devices, split_heads(): lax.psum_scatter(partial, 'fsdp', scatter_dimension=0, axis_index_groups=...  62.4 us
    ppermute x3, waiting for transfers between devices, split_heads(): pieces.append(lax.ppermute(sent, 'fsdp', pairs))  32.6 us
    unnamed x39, local copies, waits for them, and re-layouts  26.5 us
    pallas_call x1, Pallas kernels, attend(): pl.pallas_call(attend_kernel, out_shape=jax.ShapeDtypeStruct(q_lin.shape,...  25.6 us
    ppermute x12, starting transfers between devices, one_hop(): return lax.ppermute(array, 'fsdp', [(f, f + 2 * step) for f in sources])  24.7 us
  transfers between devices with their start and end apart: 23, of which 13 were waited for; matrix products, arithmetic and copies ran while one was open for 10% of the time, Pallas kernels for 0%

profile of v3, /device:TPU:0, one launch (start us, length us, event | category | flops | bytes accessed | tf_op | source)
XLA Modules:
  0.0 450.5 jit_solution(2787655791469768120)
XLA Ops:
  15.2 2.5 constant_dynamic-update-slice_fusion.13
  19.0 6.5 %collective-permute-start.6 = (bf16[2,2048,128]{2,1,0:T(8,128)(2,1)S(1)}, bf16[2,2048,128]{2,1,0:T(8,128)(2,1)}, u32[]{:S(2)}, u32[]{:S(2)}) collective-permute-start(bf16[2,2048,128]{2,1,0:T(8,128)(2,1)S(1)} %get-tuple-element.30), channel_id=1, source_target_pairs={{0,2},{1,3},{2,4},{3,5},{4,6},{5,7},{8,10},{9,11},{10,12},{11,13},... | collective-permute-start | bytes 3145736 | tf_op jit(solution)/shard_map/ppermute | solution.py:240
  25.5 2.8 constant_dynamic-update-slice_fusion.6
  29.6 5.6 %collective-permute-start.3 = (bf16[2,2048,128]{2,1,0:T(8,128)(2,1)}, bf16[2,2048,128]{2,1,0:T(8,128)(2,1)}, u32[]{:S(2)}, u32[]{:S(2)}) collective-permute-start(bf16[2,2048,128]{2,1,0:T(8,128)(2,1)} %get-tuple-element.32), channel_id=1, source_target_pairs={{0,2},{1,3},{2,4},{3,5},{4,6},{5,7},{8,10},{9,11},{10,12},{11,13},... | collective-permute-start | bytes 3145736 | tf_op jit(solution)/shard_map/ppermute | solution.py:240
  35.2 3.4 maximum_select_fusion.1
  38.6 8.7 %all-gather.2.cloned.1.call-done = bf16[256,4096]{0,1:T(8,128)(2,1)} async-done(((bf16[256,1024]{0,1:T(8,128)(2,1)}), bf16[256,4096]{0,1:T(8,128)(2,1)}) %all-gather.2.cloned.1.call-update) | async-done | bytes 2097168 | tf_op jit(solution)/shard_map/all_gather | solution.py:280
  47.3 2.3 fusion
  50.3 18.3 %collective-permute-done.4 = bf16[2,2048,128]{2,1,0:T(8,128)(2,1)} collective-permute-done((bf16[2,2048,128]{2,1,0:T(8,128)(2,1)}, bf16[2,2048,128]{2,1,0:T(8,128)(2,1)}, u32[]{:S(2)}, u32[]{:S(2)}) %collective-permute-start.4) | collective-permute-done | bytes 1048608 | tf_op jit(solution)/shard_map/ppermute | solution.py:240
  72.2 2.5 collective-permute-start.8
  74.6 3.7 collective-permute-start.9
  79.0 12.0 %collective-permute-done.8 = bf16[256,1024]{1,0:T(8,128)(2,1)S(1)} collective-permute-done((bf16[256,1024]{1,0:T(8,128)(2,1)}, bf16[256,1024]{1,0:T(8,128)(2,1)S(1)}, u32[]{:S(2)}, u32[]{:S(2)}) %collective-permute-start.8) | collective-permute-done | bytes 524320 | tf_op jit(solution)/shard_map/ppermute | solution.py:290
  91.0 20.7 %collective-permute-done.9 = bf16[256,1024]{1,0:T(8,128)(2,1)S(1)} collective-permute-done((bf16[256,1024]{1,0:T(8,128)(2,1)S(1)}, bf16[256,1024]{1,0:T(8,128)(2,1)S(1)}, u32[]{:S(2)}, u32[]{:S(2)}) %collective-permute-start.9) | collective-permute-done | bytes 524320 | tf_op jit(solution)/shard_map/ppermute | solution.py:290
  112.6 2.9 fusion.9
  129.2 2.9 maximum_select_fusion
  133.1 22.5 %collective-permute-done.13 = bf16[2,2048,128]{2,1,0:T(8,128)(2,1)S(1)} collective-permute-done((bf16[2,2048,128]{2,1,0:T(8,128)(2,1)}, bf16[2,2048,128]{2,1,0:T(8,128)(2,1)S(1)}, u32[]{:S(2)}, u32[]{:S(2)}) %collective-permute-start.13) | collective-permute-done | bytes 1048608 | tf_op jit(solution)/shard_map/ppermute | solution.py:240
  155.7 22.2 %collective-permute-done.15 = bf16[2,2048,128]{2,1,0:T(8,128)(2,1)} collective-permute-done((bf16[2,2048,128]{2,1,0:T(8,128)(2,1)}, bf16[2,2048,128]{2,1,0:T(8,128)(2,1)}, u32[]{:S(2)}, u32[]{:S(2)}) %collective-permute-start.15) | collective-permute-done | bytes 1048608 | tf_op jit(solution)/shard_map/ppermute | solution.py:240
  177.9 8.1 %fusion.12 = f32[2048,1280]{1,0:T(8,128)} fusion(bf16[2048,1024]{1,0:T(8,128)(2,1)S(1)} %bitcast.50, bf16[1024,1280]{1,0:T(8,128)(2,1)S(1)} %bitcast.51), kind=kOutput, calls=%fused_computation.76 | convolution fusion | flops 5368709120 | bytes 17301504 | tf_op jit(solution)/shard_map/dot_general | solution.py:298
  192.5 2.4 constant_dynamic-update-slice_fusion.12
  208.3 2.3 constant_dynamic-update-slice_fusion.9
  212.9 66.2 %collective-permute-done.17 = bf16[2,2048,128]{2,1,0:T(8,128)(2,1)S(1)} collective-permute-done((bf16[2,2048,128]{2,1,0:T(8,128)(2,1)S(1)}, bf16[2,2048,128]{2,1,0:T(8,128)(2,1)S(1)}, u32[]{:S(2)}, u32[]{:S(2)}) %collective-permute-start.17) | collective-permute-done | bytes 1048608 | tf_op jit(solution)/shard_map/ppermute | solution.py:240
  280.2 64.8 %collective-permute-done.19 = bf16[2,2048,128]{2,1,0:T(8,128)(2,1)S(1)} collective-permute-done((bf16[2,2048,128]{2,1,0:T(8,128)(2,1)}, bf16[2,2048,128]{2,1,0:T(8,128)(2,1)S(1)}, u32[]{:S(2)}, u32[]{:S(2)}) %collective-permute-start.19) | collective-permute-done | bytes 1048608 | tf_op jit(solution)/shard_map/ppermute | solution.py:240
  346.1 62.4 %reduce-scatter.2.cloned.1.call-done = f32[512,1280]{1,0:T(8,128)} async-done(((f32[2048,1280]{1,0:T(8,128)}), f32[512,1280]{1,0:T(8,128)}) %reduce-scatter.2.cloned.1.call-update) | async-done | bytes 2621456 | tf_op jit(solution)/shard_map/reduce_scatter | solution.py:300
  411.5 3.1 copy-done
  414.5 25.6 %shard_map.118 = bf16[512,1024]{1,0:T(8,128)(2,1)S(1)} custom-call(s32[8]{0:T(128)S(1)} %fusion.5.doc_ref, s32[8]{0:T(128)S(1)} %squeeze.37.len_ref, f32[512,1024]{1,0:T(8,128)S(1)} %slice.40.q_ref, f32[512,128]{1,0:T(8,128)S(1)} %get-tuple-element.38.k_ref, f32[512,128]{1,0:T(8,128)S(1)} %get-tuple-element.37.v_ref, f32[1,1024]{1,0:T(1,128)S(1)} %bitcast.48, ...), custom_call_target="tpu_custom_call" | custom-call | flops 4294967296 | bytes 16777216 | tf_op jit(solution)/shard_map/pallas_call | solution.py:153
  (107 shorter events, 55.2 us)
Async XLA Ops:
  6.5 40.7 %all-gather.2.cloned.1.call-start = ((), (), s32[]{:S(2)}) async-start(), calls=%async_computation.1 | async-start | bytes 2621440 | tf_op jit(solution)/shard_map/all_gather | solution.py:280
  8.8 399.8 %reduce-scatter.2.cloned.1.call-start = ((), (), s32[]{:S(2)}) async-start(), calls=%async_computation.2 | async-start | bytes 13107200 | tf_op jit(solution)/shard_map/reduce_scatter | solution.py:300
  10.9 24.2 %collective-permute-start.1 = (bf16[512,1280]{1,0:T(8,128)(2,1)S(1)}, bf16[512,1280]{1,0:T(8,128)(2,1)}, u32[]{:S(2)}, u32[]{:S(2)}) collective-permute-start(bf16[512,1280]{1,0:T(8,128)(2,1)S(1)} %pad_maximum_fusion.2), channel_id=1, source_target_pairs={{0,1},{1,0},{2,3},{3,2},{4,5},{5,4},{6,7},{7,6},{8,9},{9,8},{10,11... | collective-permute-start | bytes 3932168 | tf_op jit(solution)/shard_map/ppermute | solution.py:222
  12.8 2.4 collective-permute-start.5
  14.1 11.4 %collective-permute-start.2 = (bf16[2048,128]{1,0:T(8,128)(2,1)}, bf16[2048,128]{1,0:T(8,128)(2,1)}, u32[]{:S(2)}, u32[]{:S(2)}) collective-permute-start(bf16[2048,128]{1,0:T(8,128)(2,1)} %get-tuple-element.51), channel_id=1, source_target_pairs={{0,1},{1,0},{2,3},{3,2},{4,5},{5,4},{6,7},{7,6},{8,9},{9,8},{10,11... | collective-permute-start | bytes 1572872 | tf_op jit(solution)/shard_map/ppermute | solution.py:222
  17.7 32.6 %collective-permute-start.7 = (bf16[2,2048,128]{2,1,0:T(8,128)(2,1)S(1)}, bf16[2,2048,128]{2,1,0:T(8,128)(2,1)}, u32[]{:S(2)}, u32[]{:S(2)}) collective-permute-start(bf16[2,2048,128]{2,1,0:T(8,128)(2,1)S(1)} %get-tuple-element.30), channel_id=1, source_target_pairs={{2,0},{3,1},{4,2},{5,3},{6,4},{7,5},{10,8},{11,9},{12,10},{13,11},... | collective-permute-start | bytes 3145736 | tf_op jit(solution)/shard_map/ppermute | solution.py:240
  19.0 31.3 %collective-permute-start.6 = (bf16[2,2048,128]{2,1,0:T(8,128)(2,1)S(1)}, bf16[2,2048,128]{2,1,0:T(8,128)(2,1)}, u32[]{:S(2)}, u32[]{:S(2)}) collective-permute-start(bf16[2,2048,128]{2,1,0:T(8,128)(2,1)S(1)} %get-tuple-element.30), channel_id=1, source_target_pairs={{0,2},{1,3},{2,4},{3,5},{4,6},{5,7},{8,10},{9,11},{10,12},{11,13},... | collective-permute-start | bytes 3145736 | tf_op jit(solution)/shard_map/ppermute | solution.py:240
  28.3 40.3 %collective-permute-start.4 = (bf16[2,2048,128]{2,1,0:T(8,128)(2,1)}, bf16[2,2048,128]{2,1,0:T(8,128)(2,1)}, u32[]{:S(2)}, u32[]{:S(2)}) collective-permute-start(bf16[2,2048,128]{2,1,0:T(8,128)(2,1)} %get-tuple-element.32), channel_id=1, source_target_pairs={{2,0},{3,1},{4,2},{5,3},{6,4},{7,5},{10,8},{11,9},{12,10},{13,11},... | collective-permute-start | bytes 3145736 | tf_op jit(solution)/shard_map/ppermute | solution.py:240
  29.6 40.2 %collective-permute-start.3 = (bf16[2,2048,128]{2,1,0:T(8,128)(2,1)}, bf16[2,2048,128]{2,1,0:T(8,128)(2,1)}, u32[]{:S(2)}, u32[]{:S(2)}) collective-permute-start(bf16[2,2048,128]{2,1,0:T(8,128)(2,1)} %get-tuple-element.32), channel_id=1, source_target_pairs={{0,2},{1,3},{2,4},{3,5},{4,6},{5,7},{8,10},{9,11},{10,12},{11,13},... | collective-permute-start | bytes 3145736 | tf_op jit(solution)/shard_map/ppermute | solution.py:240
  72.2 18.8 %collective-permute-start.8 = (bf16[256,1024]{1,0:T(8,128)(2,1)}, bf16[256,1024]{1,0:T(8,128)(2,1)S(1)}, u32[]{:S(2)}, u32[]{:S(2)}) collective-permute-start(bf16[256,1024]{1,0:T(8,128)(2,1)} %bitcast.14), channel_id=1, source_target_pairs={{0,2},{1,3},{2,4},{3,5},{4,6},{5,7},{6,0},{7,1},{8,10},{9,11},{10,... | collective-permute-start | bytes 1572872 | tf_op jit(solution)/shard_map/ppermute | solution.py:290
  74.6 37.0 %collective-permute-start.9 = (bf16[256,1024]{1,0:T(8,128)(2,1)S(1)}, bf16[256,1024]{1,0:T(8,128)(2,1)S(1)}, u32[]{:S(2)}, u32[]{:S(2)}) collective-permute-start(bf16[256,1024]{1,0:T(8,128)(2,1)S(1)} %bitcast.56), channel_id=1, source_target_pairs={{0,4},{1,5},{2,6},{3,7},{4,0},{5,1},{6,2},{7,3},{8,12},{9,13},{10,... | collective-permute-start | bytes 1572872 | tf_op jit(solution)/shard_map/ppermute | solution.py:290
  78.4 33.3 %collective-permute-start.10 = (bf16[256,1024]{1,0:T(8,128)(2,1)}, bf16[256,1024]{1,0:T(8,128)(2,1)S(1)}, u32[]{:S(2)}, u32[]{:S(2)}) collective-permute-start(bf16[256,1024]{1,0:T(8,128)(2,1)} %bitcast.18), channel_id=1, source_target_pairs={{0,6},{1,7},{2,0},{3,1},{4,2},{5,3},{6,4},{7,5},{8,14},{9,15},{10,... | collective-permute-start | bytes 1572872 | tf_op jit(solution)/shard_map/ppermute | solution.py:290
  115.5 13.7 %collective-permute-start.11 = (bf16[4,256,1024]{2,1,0:T(8,128)(2,1)}, bf16[4,256,1024]{2,1,0:T(8,128)(2,1)}, u32[]{:S(2)}, u32[]{:S(2)}) collective-permute-start(bf16[4,256,1024]{2,1,0:T(8,128)(2,1)} %get-tuple-element.40), channel_id=1, source_target_pairs={{0,1},{1,0},{2,3},{3,2},{4,5},{5,4},{6,7},{7,6},{8,9},{9,8},{10,11... | collective-permute-start | bytes 6291464 | tf_op jit(solution)/shard_map/ppermute | solution.py:222
  115.6 17.6 %collective-permute-start.12 = (bf16[2,2048,128]{2,1,0:T(8,128)(2,1)}, bf16[2,2048,128]{2,1,0:T(8,128)(2,1)}, u32[]{:S(2)}, u32[]{:S(2)}) collective-permute-start(bf16[2,2048,128]{2,1,0:T(8,128)(2,1)} %collective-permute-done.3), channel_id=1, source_target_pairs={{2,4},{3,5},{4,6},{5,7},{10,12},{11,13},{12,14},{13,15},{18,20},{1... | collective-permute-start | bytes 3145736 | tf_op jit(solution)/shard_map/ppermute | solution.py:240
  117.2 38.5 %collective-permute-start.13 = (bf16[2,2048,128]{2,1,0:T(8,128)(2,1)}, bf16[2,2048,128]{2,1,0:T(8,128)(2,1)S(1)}, u32[]{:S(2)}, u32[]{:S(2)}) collective-permute-start(bf16[2,2048,128]{2,1,0:T(8,128)(2,1)} %collective-permute-done.4), channel_id=1, source_target_pairs={{2,0},{3,1},{4,2},{5,3},{10,8},{11,9},{12,10},{13,11},{18,16},{19,... | collective-permute-start | bytes 3145736 | tf_op jit(solution)/shard_map/ppermute | solution.py:240
  118.5 37.2 %collective-permute-start.14 = (bf16[2,2048,128]{2,1,0:T(8,128)(2,1)}, bf16[2,2048,128]{2,1,0:T(8,128)(2,1)}, u32[]{:S(2)}, u32[]{:S(2)}) collective-permute-start(bf16[2,2048,128]{2,1,0:T(8,128)(2,1)} %collective-permute-done.6), channel_id=1, source_target_pairs={{2,4},{3,5},{4,6},{5,7},{10,12},{11,13},{12,14},{13,15},{18,20},{1... | collective-permute-start | bytes 3145736 | tf_op jit(solution)/shard_map/ppermute | solution.py:240
  120.2 57.7 %collective-permute-start.15 = (bf16[2,2048,128]{2,1,0:T(8,128)(2,1)}, bf16[2,2048,128]{2,1,0:T(8,128)(2,1)}, u32[]{:S(2)}, u32[]{:S(2)}) collective-permute-start(bf16[2,2048,128]{2,1,0:T(8,128)(2,1)} %collective-permute-done.7), channel_id=1, source_target_pairs={{2,0},{3,1},{4,2},{5,3},{10,8},{11,9},{12,10},{13,11},{18,16},{19,... | collective-permute-start | bytes 3145736 | tf_op jit(solution)/shard_map/ppermute | solution.py:240
  132.5 45.3 %copy-start.2 = (bf16[2,512,1280]{2,1,0:T(8,128)(2,1)S(1)}, bf16[2,512,1280]{2,1,0:T(8,128)(2,1)}, u32[]{:S(2)}) copy-start(bf16[2,512,1280]{2,1,0:T(8,128)(2,1)} %maximum_select_fusion.1) | copy-start | bytes 7864324
  186.7 1.2 collective-permute-start
  189.2 13.6 %collective-permute-start.16 = (bf16[2,2048,128]{2,1,0:T(8,128)(2,1)}, bf16[2,2048,128]{2,1,0:T(8,128)(2,1)S(1)}, u32[]{:S(2)}, u32[]{:S(2)}) collective-permute-start(bf16[2,2048,128]{2,1,0:T(8,128)(2,1)} %collective-permute-done.12), channel_id=1, source_target_pairs={{4,6},{5,7},{12,14},{13,15},{20,22},{21,23},{28,30},{29,31}} | collective-permute-start | bytes 3145736 | tf_op jit(solution)/shard_map/ppermute | solution.py:240
  194.8 12.5 %collective-permute-start.18 = (bf16[2,2048,128]{2,1,0:T(8,128)(2,1)}, bf16[2,2048,128]{2,1,0:T(8,128)(2,1)S(1)}, u32[]{:S(2)}, u32[]{:S(2)}) collective-permute-start(bf16[2,2048,128]{2,1,0:T(8,128)(2,1)} %collective-permute-done.14), channel_id=1, source_target_pairs={{4,6},{5,7},{12,14},{13,15},{20,22},{21,23},{28,30},{29,31}} | collective-permute-start | bytes 3145736 | tf_op jit(solution)/shard_map/ppermute | solution.py:240
  197.8 81.3 %collective-permute-start.17 = (bf16[2,2048,128]{2,1,0:T(8,128)(2,1)S(1)}, bf16[2,2048,128]{2,1,0:T(8,128)(2,1)S(1)}, u32[]{:S(2)}, u32[]{:S(2)}) collective-permute-start(bf16[2,2048,128]{2,1,0:T(8,128)(2,1)S(1)} %collective-permute-done.13), channel_id=1, source_target_pairs={{2,0},{3,1},{10,8},{11,9},{18,16},{19,17},{26,24},{27,25}} | collective-permute-start | bytes 3145736 | tf_op jit(solution)/shard_map/ppermute | solution.py:240
  199.1 145.9 %collective-permute-start.19 = (bf16[2,2048,128]{2,1,0:T(8,128)(2,1)}, bf16[2,2048,128]{2,1,0:T(8,128)(2,1)S(1)}, u32[]{:S(2)}, u32[]{:S(2)}) collective-permute-start(bf16[2,2048,128]{2,1,0:T(8,128)(2,1)} %collective-permute-done.15), channel_id=1, source_target_pairs={{2,0},{3,1},{10,8},{11,9},{18,16},{19,17},{26,24},{27,25}} | collective-permute-start | bytes 3145736 | tf_op jit(solution)/shard_map/ppermute | solution.py:240
  440.3 2.0 collective-permute-start.20
  (13 other events, 33.0 us)
Sparse Core Ops, SparseCore 0:
  9.2 38.0 all-gather.1
  186.2 222.3 reduce-scatter.1
